TPU v7x, 256 devices: a whole 4x4x8 slice. The times are simulated.
256 devices in a mesh: leaf: 32 (over z, x), gx: 2 (over core), gy: 4 (over y).
Axes of the slice: x: 4, y: 4, z: 8, core: 2. Of those that a mesh axis runs over, the one named last changes fastest.
Arguments:
- leaf_rhs: float32 [32, 2, 4, 48, 16, 128], P('leaf', 'gx', 'gy'), may hold values from -6 to 6
- leaf_inv: float32 [32, 2, 4, 48, 128, 128], P('leaf', 'gx', 'gy'), may hold values from -0.4 to 1.7
- edge_blocks: float32 [32, 2, 4, 48, 2, 128, 128], P('leaf', 'gx', 'gy'), may hold values from -0.09375 to 0.09375
- edge_target: int32 [32, 2, 4, 48, 2], P('leaf', 'gx', 'gy'), may hold values from 0 to 639
- sep_rhs: float32 [32, 2, 4, 4, 16, 128], P('leaf', 'gx', 'gy'), may hold values from -6 to 6
- sep_inv: float32 [32, 2, 4, 4, 128, 128], P('leaf', 'gx', 'gy'), may hold values from -0.4 to 1.7
- sep_up: float32 [32, 2, 4, 4, 128, 128], P('leaf', 'gx', 'gy'), may hold values from -0.4375 to 0.4375
- sep_parent: int32 [32, 2, 4, 4], P('leaf', 'gx', 'gy'), may hold values from 0 to 3
Outputs:
- leaf_solution: float32 [32, 2, 4, 48, 16, 128], P('leaf', 'gx', 'gy')
- sep_solution: float32 [32, 2, 4, 4, 16, 128], P('leaf', 'gx', 'gy')
All inputs are finite; a program needn't handle non-finite values.
Results may differ from a plain program's by a relative error of at most 0.0003.
Values sent between devices are 32-bit elements; how exact they have to be, the bound alone decides.
No kernel may reach another device: no remote copies, remote signals or barrier semaphores. Data moves between devices by JAX's collectives and lax.ppermute only.
A program may use at most 64 MiB of HBM per device.

v0:
```python
import jax
import jax.numpy as jnp
from jax import lax
from jax.sharding import PartitionSpec as P

HIGHEST = lax.Precision.HIGHEST


def from_behind(value, axis, steps):
    count = lax.axis_size(axis)
    initial, last = (max(0, -steps), min(count, count - steps))
    return lax.ppermute(value, axis, [(source, source + steps) for source in range(initial, last)])


def extended(block, sides, width):
    for axis, dim in sides:
        count = lax.axis_size(axis)
        forward = [(i, i + 1) for i in range(count - 1)]
        backward = [(target, source) for source, target in forward]
        low = lax.ppermute(
            lax.slice_in_dim(block, block.shape[dim] - width, None, axis=dim), axis, forward
        )
        high = lax.ppermute(lax.slice_in_dim(block, 0, width, axis=dim), axis, backward)
        block = jnp.concatenate([low, block, high], axis=dim)
    return block


def along_rows(value, offset):
    return from_behind(value, "gx", offset)


def along_cols(value, offset):
    return from_behind(value, "gy", offset)


def along_levels(value, offset):
    return from_behind(value, "leaf", offset)


def local(leaf_rhs, leaf_inv, edge_blocks, edge_target, sep_rhs, sep_inv, sep_up, sep_parent):
    levels = lax.axis_size("leaf")
    rhs_leaf = leaf_rhs[0, 0, 0]
    inv_leaf = leaf_inv[0, 0, 0]
    blocks = edge_blocks[0, 0, 0]
    target = edge_target[0, 0, 0]
    rhs_sep = sep_rhs[0, 0, 0]
    inv_sep = sep_inv[0, 0, 0]
    up_blocks = sep_up[0, 0, 0]
    parent = sep_parent[0, 0, 0]
    slot_count, rhs_cols, block_width = rhs_leaf.shape
    sep_count = rhs_sep.shape[0]
    targets = 5 * levels * sep_count
    leaf_mid = jnp.einsum("srw,svw->srv", rhs_leaf, inv_leaf, precision=HIGHEST)
    products = jnp.einsum("srw,skvw->skrv", leaf_mid, blocks, precision=HIGHEST)
    chosen = (target[:, :, None] == jnp.arange(targets, dtype=jnp.int32)).astype(jnp.float32)
    outgoing = jnp.einsum("skt,skrv->trv", chosen, products, precision=HIGHEST)
    outgoing = outgoing.reshape(5, levels, sep_count, rhs_cols, block_width)
    arriving = outgoing[0] + along_rows(outgoing[2], 1) + along_rows(outgoing[1], -1)
    arriving = arriving + along_cols(outgoing[4], 1) + along_cols(outgoing[3], -1)
    updates = lax.psum_scatter(arriving, "leaf", scatter_dimension=0, tiled=True)[0]
    reduced = rhs_sep - updates
    parent_pick = (parent[:, None] == jnp.arange(sep_count, dtype=jnp.int32)).astype(jnp.float32)

    def solve_up(incoming):
        partial_mid = jnp.einsum("srw,svw->srv", reduced - incoming, inv_sep, precision=HIGHEST)
        lifted = jnp.einsum("crw,cvw->crv", partial_mid, up_blocks, precision=HIGHEST)
        return (partial_mid, jnp.einsum("cp,crv->prv", parent_pick, lifted, precision=HIGHEST))

    def solve_down(sep_mid, from_above):
        parents = jnp.einsum("cp,prw->crw", parent_pick, from_above, precision=HIGHEST)
        pushed = jnp.einsum("crv,cvw->crw", parents, up_blocks, precision=HIGHEST)
        return jnp.einsum("srv,svw->srw", sep_mid - pushed, inv_sep, precision=HIGHEST)

    empty = jnp.zeros_like(rhs_sep)

    def forward_step(turn, incoming):
        return along_levels(solve_up(incoming)[1], 1)

    incoming = lax.fori_loop(0, levels - 1, forward_step, empty)
    sep_mid = solve_up(incoming)[0]

    def backward_step(turn, from_above):
        return along_levels(solve_down(sep_mid, from_above), -1)

    from_above = lax.fori_loop(0, levels - 1, backward_step, empty)
    sep_sol = solve_down(sep_mid, from_above)
    every_level = lax.all_gather(sep_sol[None], "leaf", axis=0, tiled=True)
    padded = extended(every_level[None, None], (("gx", 0), ("gy", 1)), 1)
    solved_table = jnp.stack([padded[1, 1], padded[0, 1], padded[2, 1], padded[1, 0], padded[1, 2]])
    solved_table = solved_table.reshape(targets, rhs_cols * block_width)
    reached = jnp.dot(chosen.reshape(-1, targets), solved_table, precision=HIGHEST)
    reached = reached.reshape(slot_count, -1, rhs_cols, block_width)
    pulled_back = jnp.einsum("skrv,skvw->srw", reached, blocks, precision=HIGHEST)
    leaf_sol = jnp.einsum("srv,svw->srw", leaf_mid - pulled_back, inv_leaf, precision=HIGHEST)
    return (leaf_sol[None, None, None], sep_sol[None, None, None])


def solution(mesh):
    in_specs = (
        P("leaf", "gx", "gy", None, None, None),
        P("leaf", "gx", "gy", None, None, None),
        P("leaf", "gx", "gy", None, None, None, None),
        P("leaf", "gx", "gy", None, None),
        P("leaf", "gx", "gy", None, None, None),
        P("leaf", "gx", "gy", None, None, None),
        P("leaf", "gx", "gy", None, None, None),
        P("leaf", "gx", "gy", None),
    )
    out_specs = (P("leaf", "gx", "gy", None, None, None), P("leaf", "gx", "gy", None, None, None))
    return jax.shard_map(local, mesh=mesh, in_specs=in_specs, out_specs=out_specs, check_vma=False)
```

profile of v0, /device:TPU:1, one launch (start us, length us, event | category | flops | bytes accessed | tf_op | source)
XLA Modules:
  0.0 1161.4 jit_solution(9223311347620786621)
XLA Ops:
  15.0 7.4 fusion.24
  40.8 10.1 collective-permute-done.5
  54.5 219.2 %reduce-scatter.2.cloned.1.call-done = f32[1,4,16,128]{3,2,1,0:T(8,128)} async-done(((f32[32,4,16,128]{3,2,1,0:T(8,128)}), f32[1,4,16,128]{3,2,1,0:T(8,128)}) %reduce-scatter.2.cloned.1.call-update) | async-done | bytes 32784 | tf_op jit(solution)/shard_map/reduce_scatter | solution.py:60
  274.6 267.6 %while.22 = (s32[]{:T(128)}, f32[4,16,128]{2,0,1:T(4,128)S(1)}, f32[4,16,128]{2,0,1:T(4,128)S(1)}, f32[4,128,128]{2,1,0:T(8,128)S(1)}, f32[4,128,128]{2,1,0:T(8,128)}, /*index=5*/s32[4]{0:T(128)S(1)}, s32[]{:T(128)}) while((s32[]{:T(128)}, f32[4,16,128]{2,0,1:T(4,128)S(1)}, f32[4,16,128]{2,0,1:T(4,128)S(1)}, ...), condition=%wide.region_2.0_spmd.clone, body=%wide.region_1.0_spmd.clone.sunk | while | flops 25567264 | bytes 950405 | solution.py:79
  408.9 6.1 collective-permute-start
  490.2 6.1 collective-permute-start
  542.6 296.4 %while.23 = (s32[]{:T(128)}, f32[4,16,128]{2,1,0:T(8,128)S(1)}, f32[4,128,128]{2,1,0:T(8,128)}, f32[4,16,128]{2,1,0:T(8,128)S(1)}, f32[4,128,128]{2,1,0:T(8,128)S(1)}, /*index=5*/s32[4]{0:T(128)S(1)}, s32[]{:T(128)}) while((s32[]{:T(128)}, f32[4,16,128]{2,1,0:T(8,128)S(1)}, f32[4,128,128]{2,1,0:T(8,128)}, ...), condition=%wide.region_4.0_spmd.clone, body=%wide.region_3.0_spmd.clone.sunk | while | flops 25567264 | bytes 884869 | solution.py:85
  572.8 6.1 collective-permute-done.1
  634.3 6.1 collective-permute-done.1
  643.5 7.0 collective-permute-done.1
  653.6 6.8 collective-permute-done.1
  663.6 7.4 collective-permute-done.1
  674.2 6.7 collective-permute-done.1
  684.0 7.3 collective-permute-done.1
  694.5 6.9 collective-permute-done.1
  704.5 6.4 collective-permute-done.1
  714.1 6.3 collective-permute-done.1
  723.6 6.5 collective-permute-done.1
  733.2 7.2 collective-permute-done.1
  743.6 6.1 collective-permute-done.1
  752.9 6.8 collective-permute-done.1
  762.9 7.1 collective-permute-done.1
  773.2 6.4 collective-permute-done.1
  782.8 7.0 collective-permute-done.1
  793.0 6.8 collective-permute-done.1
  802.9 6.3 collective-permute-done.1
  812.4 6.7 collective-permute-done.1
  822.3 7.2 collective-permute-done.1
  832.7 6.4 collective-permute-done.1
  841.5 200.2 %all-gather.3.cloned.1.call-done = f32[128,16,128]{2,1,0:T(8,128)} async-done(((f32[4,16,128]{2,1,0:T(8,128)}), f32[128,16,128]{2,1,0:T(8,128)}) %all-gather.3.cloned.1.call-update) | async-done | bytes 1048592 | tf_op jit(solution)/shard_map/all_gather | solution.py:87
  1043.2 7.8 collective-permute-start.7
  1059.8 65.3 %collective-permute-done.8 = f32[3,1,32,4,16,128]{5,4,3,2,1,0:T(8,128)S(1)} collective-permute-done((f32[3,1,32,4,16,128]{5,4,3,2,1,0:T(8,128)S(1)}, f32[3,1,32,4,16,128]{5,4,3,2,1,0:T(8,128)S(1)}, u32[]{:S(2)}, u32[]{:S(2)}) %collective-permute-start.8) | collective-permute-done | bytes 3145760 | tf_op jit(solution)/shard_map/ppermute | solution.py:20
  (377 shorter events, 476.0 us)
Async XLA Ops:
  7.2 266.6 %reduce-scatter.2.cloned.1.call-start = ((), (), s32[]{:S(2)}) async-start(), calls=%async_computation.1 | async-start | bytes 1081344 | tf_op jit(solution)/shard_map/reduce_scatter | solution.py:60
  26.2 24.7 %collective-permute-start.5 = (f32[32,4,16,128]{3,2,1,0:T(8,128)S(1)}, f32[32,4,16,128]{3,2,1,0:T(8,128)S(1)}, u32[]{:S(2)}, u32[]{:S(2)}) collective-permute-start(f32[32,4,16,128]{3,2,1,0:T(8,128)S(1)} %copy.53), channel_id=1, source_target_pairs={{1,0},{2,1},{3,2},{5,4},{6,5},{7,6},{9,8},{10,9},{11,10},{13,12},{... | collective-permute-start | bytes 3145736 | tf_op jit(solution)/shard_map/ppermute | solution.py:12
  28.2 24.3 %collective-permute-start.4 = (f32[32,4,16,128]{3,2,1,0:T(8,128)S(1)}, f32[32,4,16,128]{3,2,1,0:T(8,128)S(1)}, u32[]{:S(2)}, u32[]{:S(2)}) collective-permute-start(f32[32,4,16,128]{3,2,1,0:T(8,128)S(1)} %copy.52), channel_id=1, source_target_pairs={{0,1},{1,2},{2,3},{4,5},{5,6},{6,7},{8,9},{9,10},{10,11},{12,13},{... | collective-permute-start | bytes 3145736 | tf_op jit(solution)/shard_map/ppermute | solution.py:12
  33.5 19.0 %collective-permute-start.3 = (f32[32,4,16,128]{3,2,1,0:T(8,128)S(1)}, f32[32,4,16,128]{3,2,1,0:T(8,128)S(1)}, u32[]{:S(2)}, u32[]{:S(2)}) collective-permute-start(f32[32,4,16,128]{3,2,1,0:T(8,128)S(1)} %copy.51), channel_id=1, source_target_pairs={{4,0},{5,1},{6,2},{7,3},{12,8},{13,9},{14,10},{15,11},{20,16},{21,... | collective-permute-start | bytes 3145736 | tf_op jit(solution)/shard_map/ppermute | solution.py:12
  39.4 13.1 %collective-permute-start.2 = (f32[32,4,16,128]{3,2,1,0:T(8,128)S(1)}, f32[32,4,16,128]{3,2,1,0:T(8,128)S(1)}, u32[]{:S(2)}, u32[]{:S(2)}) collective-permute-start(f32[32,4,16,128]{3,2,1,0:T(8,128)S(1)} %copy.49), channel_id=1, source_target_pairs={{0,4},{1,5},{2,6},{3,7},{8,12},{9,13},{10,14},{11,15},{16,20},{17,... | collective-permute-start | bytes 3145736 | tf_op jit(solution)/shard_map/ppermute | solution.py:12
  54.5 987.3 %all-gather.3.cloned.1.call-start = ((), (), s32[]{:S(2)}) async-start(), calls=%async_computation.2 | async-start | bytes 1081344 | tf_op jit(solution)/shard_map/all_gather | solution.py:87
  571.5 7.4 collective-permute-start.1
  633.0 7.4 collective-permute-start.1
  642.2 8.3 collective-permute-start.1
  652.3 8.1 collective-permute-start.1
  662.3 8.7 collective-permute-start.1
  672.9 8.0 collective-permute-start.1
  682.7 8.6 collective-permute-start.1
  693.2 8.2 collective-permute-start.1
  703.2 7.7 collective-permute-start.1
  712.8 7.6 collective-permute-start.1
  722.3 7.8 collective-permute-start.1
  731.9 8.5 collective-permute-start.1
  742.3 7.4 collective-permute-start.1
  751.6 8.1 collective-permute-start.1
  761.6 8.4 collective-permute-start.1
  771.9 7.7 collective-permute-start.1
  781.5 8.3 collective-permute-start.1
  791.7 8.1 collective-permute-start.1
  801.6 7.6 collective-permute-start.1
  811.1 8.0 collective-permute-start.1
  821.0 8.5 collective-permute-start.1
  831.4 7.7 collective-permute-start.1
  1041.8 9.5 collective-permute-start.6
  1043.2 10.2 collective-permute-start.7
  1055.0 70.2 %collective-permute-start.8 = (f32[3,1,32,4,16,128]{5,4,3,2,1,0:T(8,128)S(1)}, f32[3,1,32,4,16,128]{5,4,3,2,1,0:T(8,128)S(1)}, u32[]{:S(2)}, u32[]{:S(2)}) collective-permute-start(f32[3,1,32,4,16,128]{5,4,3,2,1,0:T(8,128)S(1)} %pad_maximum_fusion), channel_id=1, source_target_pairs={{0,1},{1,2},{2,3},{4,5},{5,6},{6,7},{8,9},{9,10},{10,11},{12,13},{... | collective-permute-start | bytes 9437192 | tf_op jit(solution)/shard_map/ppermute | solution.py:20
  1058.3 70.9 %collective-permute-start.9 = (f32[3,1,32,4,16,128]{5,4,3,2,1,0:T(8,128)S(1)}, f32[3,1,32,4,16,128]{5,4,3,2,1,0:T(8,128)S(1)}, u32[]{:S(2)}, u32[]{:S(2)}) collective-permute-start(f32[3,1,32,4,16,128]{5,4,3,2,1,0:T(8,128)S(1)} %pad_maximum_fusion), channel_id=1, source_target_pairs={{1,0},{2,1},{3,2},{5,4},{6,5},{7,6},{9,8},{10,9},{11,10},{13,12},{... | collective-permute-start | bytes 9437192 | tf_op jit(solution)/shard_map/ppermute | solution.py:23
  (48 other events, 1031.8 us)
Sparse Core Ops, SparseCore 0:
  54.6 219.0 reduce-scatter.1
  841.7 200.0 all-gather.2
where the time goes:
time: 1170 us; the launch traced here: 1160 us
  waiting for transfers between devices  732 us (63%)
  starting transfers between devices  234 us (20%)
  matrix products  159 us (14%)
  local copies, waits for them, and re-layouts  16.1 us (1%)
  between operations  14.3 us (1%)
    ppermute x66, waiting for transfers between devices, from_behind(): lax.ppermute(value, axis, [(source, source + steps) for source in range(i...  241 us
    ppermute x66, starting transfers between devices, from_behind(): lax.ppermute(value, axis, [(source, source + steps) for source in range(i...  220 us
    reduce_scatter x1, waiting for transfers between devices, local(): lax.psum_scatter(arriving, 'leaf', scatter_dimension=0, tiled=True)[0]  219 us
    all_gather x1, waiting for transfers between devices, local(): every_level = lax.all_gather(sep_sol[None], 'leaf', axis=0, tiled=True)  200 us
    ppermute x2, waiting for transfers between devices, extended(): lax.ppermute(lax.slice_in_dim(block, block.shape[dim] - width, None, axis...  65.6 us
    dot_general x31, matrix products, solve_up(): jnp.einsum('crw,cvw->crv', partial_mid, up_blocks, precision=HIGHEST)  45.6 us
    dot_general x32, matrix products, solve_down(): pushed = jnp.einsum('crv,cvw->crw', parents, up_blocks, precision=HIGHEST)  40.8 us
  transfers between devices with their start and end apart: 72, of which 70 were waited for; matrix products, arithmetic and copies ran while one was open for 0% of the time, Pallas kernels for 0%

commit v1 on v0

v1 whole, which is shorter than its diff:
```python
import functools

import jax
import jax.numpy as jnp
from jax import lax
from jax.experimental import pallas as pl
from jax.experimental.pallas import tpu as pltpu
from jax.sharding import PartitionSpec as P

F32 = jnp.float32
BF16 = jnp.bfloat16
W = 128
R = 16
SEP = 4
NX = 4
NZ = 8
STEP = 4
NN = (((1,), (0,)), ((), ()))
NT = (((1,), (1,)), ((), ()))
TN = (((0,), (0,)), ((), ()))

X_GROUPS = [[z * NX + x for x in range(NX)] for z in range(NZ)]
Z_GROUPS = [[z * NX + x for z in range(NZ)] for x in range(NX)]


def along_x(value, offset):
    pairs = [(z * NX + x, z * NX + (x + offset) % NX) for z in range(NZ) for x in range(NX)]
    return lax.ppermute(value, "leaf", pairs)


def along_z(value, offset):
    pairs = [(z * NX + x, ((z + offset) % NZ) * NX + x) for z in range(NZ) for x in range(NX)]
    return lax.ppermute(value, "leaf", pairs)


def along_y(value, offset):
    count = lax.axis_size("gy")
    return lax.ppermute(value, "gy", [(i, i + offset) for i in range(count) if 0 <= i + offset < count])


def swap_x(value):
    return lax.ppermute(value, "gx", [(0, 1), (1, 0)])


def parts(value):
    high = value.astype(BF16).astype(F32)
    return high, value - high


def rows_of(value):
    return jnp.concatenate(parts(value), axis=0).astype(BF16)


def cols_of(value):
    return jnp.concatenate(parts(value), axis=1).astype(BF16)


def folded(out, rows):
    out = out[:, :W] + out[:, W:]
    return out[:rows] + out[rows:]


def times(left, dims, right):
    out = lax.dot_general(rows_of(left), right, dims, preferred_element_type=F32)
    return folded(out, left.shape[0])


def leaf_up_kernel(idx_ref, own_ref, rhs_ref, inv_ref, edge_ref, sep_ref, mid_ref, prod_ref, acc_ref):
    step = pl.program_id(0)

    @pl.when(step == 0)
    def _():
        acc_ref[...] = jnp.zeros_like(acc_ref)
        for s in range(SEP):
            acc_ref[own_ref[0] * SEP + s] = -sep_ref[s]

    for s in range(STEP):
        mid = times(rhs_ref[s], NT, rows_of(inv_ref[s]))
        mid_ref[s] = mid
        for j in range(2):
            product = times(mid, NT, rows_of(edge_ref[s, j]))
            prod_ref[2 * s + j] = product
            at = idx_ref[(step * STEP + s) * 2 + j]
            acc_ref[at] += product


def leaf_up(idx, own, rhs, inv, edges, sep_rhs):
    count = rhs.shape[0]
    spec = pltpu.PrefetchScalarGridSpec(
        num_scalar_prefetch=2,
        grid=(count // STEP,),
        in_specs=[
            pl.BlockSpec((STEP, R, W), lambda i, *_: (i, 0, 0)),
            pl.BlockSpec((STEP, W, W), lambda i, *_: (i, 0, 0)),
            pl.BlockSpec((STEP, 2, W, W), lambda i, *_: (i, 0, 0, 0)),
            pl.BlockSpec((SEP, R, W), lambda i, *_: (0, 0, 0)),
        ],
        out_specs=[
            pl.BlockSpec((STEP, R, W), lambda i, *_: (i, 0, 0)),
            pl.BlockSpec((2 * STEP, R, W), lambda i, *_: (i, 0, 0)),
            pl.BlockSpec((NX * NZ * SEP + 1, R, W), lambda i, *_: (0, 0, 0)),
        ],
    )
    return pl.pallas_call(
        leaf_up_kernel,
        grid_spec=spec,
        out_shape=[
            jax.ShapeDtypeStruct((count, R, W), F32),
            jax.ShapeDtypeStruct((2 * count, R, W), F32),
            jax.ShapeDtypeStruct((NX * NZ * SEP + 1, R, W), F32),
        ],
        cost_estimate=pl.CostEstimate(flops=10**9, bytes_accessed=12 * 10**6, transcendentals=0),
        name="leaf_up",
    )(idx, own, rhs, inv, edges, sep_rhs)


def collect_kernel(idx_ref, acc_ref, a_ref, b_ref, c_ref, out_ref, sums):
    sums[...] = acc_ref[...]
    count = a_ref.shape[0]

    def add(i, carry):
        for m in range(4):
            n = i * 4 + m
            sums[idx_ref[n]] += a_ref[n]
            sums[idx_ref[count + n]] += b_ref[n]
            sums[idx_ref[2 * count + n]] += c_ref[n]
        return carry

    lax.fori_loop(0, count // 4, add, 0)

    def place(z, carry):
        for k in range(NX * SEP):
            tile = sums[z * NX * SEP + k]
            for x in range(NX):
                out_ref[z * NX + x, k] = tile[4 * x : 4 * x + 4]
        return carry

    lax.fori_loop(0, NZ, place, 0)


def vmem():
    return pl.BlockSpec(memory_space=pltpu.VMEM)


def smem():
    return pl.BlockSpec(memory_space=pltpu.SMEM)


def collect(idx, acc, a, b, c):
    return pl.pallas_call(
        collect_kernel,
        in_specs=[smem()] + [vmem()] * 4,
        out_specs=vmem(),
        out_shape=jax.ShapeDtypeStruct((NX * NZ, NX * SEP, R // NX, W), F32),
        scratch_shapes=[pltpu.VMEM(acc.shape, F32)],
        cost_estimate=pl.CostEstimate(flops=10**6, bytes_accessed=5 * 10**6, transcendentals=0),
        name="collect",
    )(idx, acc, a, b, c)


def picked(rows, c, p):
    return rows[c : c + 1, :] == float(p)


def blocks_kernel(me_ref, p0_ref, p1_ref, p2_ref, p3_ref, bt_ref, bn_ref, g_ref, par_ref, comp_ref):
    me = me_ref[0]
    sources = (p0_ref, p1_ref, p2_ref, p3_ref)
    for o in range(NX):
        level = lax.rem(me - o + NX, NX)
        ref = sources[o]
        for c in range(SEP):
            inv = ref[c * W : (c + 1) * W]
            up = ref[(SEP + c) * W : (SEP + c + 1) * W]
            inv_rows = parts(inv)
            inv_cols = jnp.concatenate(inv_rows, axis=1).astype(BF16)
            normal = times(up, NN, inv_cols)
            bn_ref[level * SEP + c] = cols_of(normal)
            flipped = lax.dot_general(inv_cols, rows_of(up), (((0,), (1,)), ((), ())), preferred_element_type=F32)
            bt_ref[level * SEP + c] = cols_of(folded(flipped, W))
            gram = lax.dot_general(inv_cols, inv_cols, TN, preferred_element_type=F32)
            g_ref[level * SEP + c] = cols_of(folded(gram, W))
        par_ref[level] = ref[2 * SEP * W :]

    def joined(c):
        pair = bn_ref[c].astype(F32)
        return pair[:, :W] + pair[:, W:]

    comp = [joined(c) for c in range(SEP)]
    to = par_ref[0]
    for j in range(1, NX):
        mats = [joined(j * SEP + p) for p in range(SEP)]
        own = par_ref[j]
        following = []
        for c in range(SEP):
            mat = mats[SEP - 1]
            row = own[SEP - 1 : SEP]
            for p in range(SEP - 1):
                mat = jnp.where(picked(to, c, p), mats[p], mat)
                row = jnp.where(picked(to, c, p), own[p : p + 1], row)
            comp[c] = times(mat, NN, cols_of(comp[c]))
            following.append(row)
        to = jnp.concatenate(following + [own[SEP:]], axis=0)
    for c in range(SEP):
        comp_ref[c * W : (c + 1) * W] = comp[c]
    comp_ref[SEP * W :] = to


def blocks(me, p0, p1, p2, p3):
    n = NX * SEP
    return pl.pallas_call(
        blocks_kernel,
        in_specs=[smem()] + [vmem()] * 4,
        out_specs=[vmem()] * 5,
        out_shape=[
            jax.ShapeDtypeStruct((n, W, 2 * W), BF16),
            jax.ShapeDtypeStruct((n, W, 2 * W), BF16),
            jax.ShapeDtypeStruct((n, W, 2 * W), BF16),
            jax.ShapeDtypeStruct((NX, 8, W), F32),
            jax.ShapeDtypeStruct((SEP * W + 8, W), F32),
        ],
        cost_estimate=pl.CostEstimate(flops=10**9, bytes_accessed=5 * 10**6, transcendentals=0),
        name="blocks",
    )(me, p0, p1, p2, p3)


def chain_prep_kernel(*refs):
    ins, (ct_ref, cn_ref, par_ref) = refs[: NZ - 1], refs[NZ - 1 :]
    for o in range(1, NZ):
        ref = ins[o - 1]
        for c in range(SEP):
            mat = ref[c * W : (c + 1) * W]
            cn_ref[o * SEP + c] = cols_of(mat)
            ct_ref[o * SEP + c] = cols_of(mat.T)
        par_ref[o] = ref[SEP * W :]


def chain_prep(others):
    n = NZ * SEP
    return pl.pallas_call(
        chain_prep_kernel,
        in_specs=[vmem()] * (NZ - 1),
        out_specs=[vmem()] * 3,
        out_shape=[
            jax.ShapeDtypeStruct((n, W, 2 * W), BF16),
            jax.ShapeDtypeStruct((n, W, 2 * W), BF16),
            jax.ShapeDtypeStruct((NZ, 8, W), F32),
        ],
        cost_estimate=pl.CostEstimate(flops=10**6, bytes_accessed=6 * 10**6, transcendentals=0),
        name="chain_prep",
    )(*others)


def lift(values, mats, base, parents):
    lifted = [times(values[c], NN, mats[base + c]) for c in range(SEP)]
    sums = []
    for p in range(SEP):
        total = jnp.where(picked(parents, 0, p), lifted[0], 0.0)
        for c in range(1, SEP):
            total = total + jnp.where(picked(parents, c, p), lifted[c], 0.0)
        sums.append(total)
    return sums


def lower(values, mats, base, parents):
    out = []
    for c in range(SEP):
        mine = values[SEP - 1]
        for p in range(SEP - 1):
            mine = jnp.where(picked(parents, c, p), values[p], mine)
        out.append(times(mine, NN, mats[base + c]))
    return out


def gather_kernel(got_ref, bt_ref, par_ref, d_ref, a_ref):
    d = got_ref[0]
    for n in range(1, NX * NZ):
        d = d + got_ref[n]
    d_ref[...] = -d
    incoming = [jnp.zeros((R // NX, W), F32)] * SEP
    for j in range(NX):
        values = [d_ref[j * SEP + c] - incoming[c] for c in range(SEP)]
        incoming = lift(values, bt_ref, j * SEP, par_ref[j])
    for c in range(SEP):
        a_ref[c] = incoming[c]


def up_kernel(me_ref, d_ref, all_ref, ct_ref, cpar_ref, bt_ref, bn_ref, g_ref, par_ref, z_ref, e_ref):
    me = me_ref[0]

    def follow(b, incoming):
        o = me - b
        moved = lift(incoming, ct_ref, o * SEP, cpar_ref[o])
        return [all_ref[b, c] + moved[c] for c in range(SEP)]

    incoming = lax.fori_loop(0, me, follow, [jnp.zeros((R // NX, W), F32)] * SEP)
    for j in range(NX):
        values = [d_ref[j * SEP + c] - incoming[c] for c in range(SEP)]
        for c in range(SEP):
            z_ref[j * SEP + c] = times(values[c], NN, g_ref[j * SEP + c])
        if j < NX - 1:
            incoming = lift(values, bt_ref, j * SEP, par_ref[j])
    above = [z_ref[(NX - 1) * SEP + c] for c in range(SEP)]
    for j in range(NX - 2, -1, -1):
        pushed = lower(above, bn_ref, j * SEP, par_ref[j])
        above = [z_ref[j * SEP + c] - pushed[c] for c in range(SEP)]
    for c in range(SEP):
        e_ref[c] = above[c]


def down_kernel(me_ref, z_ref, all_ref, cn_ref, cpar_ref, bn_ref, par_ref, sol_ref):
    me = me_ref[0]

    def follow(i, above):
        b = NZ - 1 - i
        o = me - b + NZ
        moved = lower(above, cn_ref, o * SEP, cpar_ref[o])
        return [all_ref[b, c] + moved[c] for c in range(SEP)]

    above = lax.fori_loop(0, NZ - 1 - me, follow, [jnp.zeros((R // NX, W), F32)] * SEP)
    for j in range(NX - 1, -1, -1):
        pushed = lower(above, bn_ref, j * SEP, par_ref[j])
        above = [z_ref[j * SEP + c] - pushed[c] for c in range(SEP)]
        for c in range(SEP):
            sol_ref[j * SEP + c] = above[c]


def chain_call(kernel, scalars, name, out_shape, *args):
    return pl.pallas_call(
        kernel,
        in_specs=[smem()] * scalars + [vmem()] * (len(args) - scalars),
        out_specs=jax.tree.map(lambda _: vmem(), out_shape),
        out_shape=out_shape,
        cost_estimate=pl.CostEstimate(flops=10**8, bytes_accessed=4 * 10**6, transcendentals=0),
        name=name,
    )(*args)


def leaf_down_kernel(idx_ref, mid_ref, inv_ref, edge_ref, own_ref, xs_ref, ym_ref, yp_ref, out_ref, table):
    step = pl.program_id(0)

    @pl.when(step == 0)
    def _():
        for n, ref in enumerate((own_ref, xs_ref, ym_ref, yp_ref)):

            def place(z, carry):
                for k in range(NX * SEP):
                    tile = jnp.concatenate([ref[z * NX + x, k] for x in range(NX)], axis=0)
                    table[(n * NZ + z) * NX * SEP + k] = tile
                return carry

            lax.fori_loop(0, NZ, place, 0)
        table[4 * NZ * NX * SEP] = jnp.zeros((R, W), F32)

    for s in range(STEP):
        at = (step * STEP + s) * 2
        pulled = times(table[idx_ref[at]], NN, cols_of(edge_ref[s, 0]))
        pulled = pulled + times(table[idx_ref[at + 1]], NN, cols_of(edge_ref[s, 1]))
        out_ref[s] = times(mid_ref[s] - pulled, NN, cols_of(inv_ref[s]))


def leaf_down(idx, mid, inv, edges, own, xs, ym, yp):
    count = mid.shape[0]
    whole = pl.BlockSpec(own.shape, lambda i, *_: (0, 0, 0, 0), pipeline_mode=pl.Buffered(1))
    spec = pltpu.PrefetchScalarGridSpec(
        num_scalar_prefetch=1,
        grid=(count // STEP,),
        in_specs=[
            pl.BlockSpec((STEP, R, W), lambda i, *_: (i, 0, 0)),
            pl.BlockSpec((STEP, W, W), lambda i, *_: (i, 0, 0)),
            pl.BlockSpec((STEP, 2, W, W), lambda i, *_: (i, 0, 0, 0)),
            whole,
            whole,
            whole,
            whole,
        ],
        out_specs=pl.BlockSpec((STEP, R, W), lambda i, *_: (i, 0, 0)),
        scratch_shapes=[pltpu.VMEM((4 * NZ * NX * SEP + 1, R, W), F32)],
    )
    return pl.pallas_call(
        leaf_down_kernel,
        grid_spec=spec,
        out_shape=jax.ShapeDtypeStruct((count, R, W), F32),
        cost_estimate=pl.CostEstimate(flops=10**9, bytes_accessed=14 * 10**6, transcendentals=0),
        name="leaf_down",
    )(idx, mid, inv, edges, own, xs, ym, yp)


def spread(value, groups=None, count=NX * NZ):
    copies = jnp.broadcast_to(value[None], (count,) + value.shape)
    return lax.all_to_all(copies, "leaf", 0, 0, axis_index_groups=groups)


def local(leaf_rhs, leaf_inv, edge_blocks, edge_target, sep_rhs, sep_inv, sep_up, sep_parent):
    rhs_leaf = leaf_rhs[0, 0, 0]
    inv_leaf = leaf_inv[0, 0, 0]
    blocks_leaf = edge_blocks[0, 0, 0]
    codes = edge_target[0, 0, 0].reshape(-1)
    rhs_sep = sep_rhs[0, 0, 0]
    level = lax.axis_index("leaf").astype(jnp.int32)
    my_x = lax.rem(level, NX).reshape(1)
    my_z = lax.div(level, NX).reshape(1)
    gx = lax.axis_index("gx").astype(jnp.int32)
    gy = lax.axis_index("gy").astype(jnp.int32)
    table = NX * NZ * SEP

    parent_rows = jnp.broadcast_to(sep_parent[0, 0, 0].astype(F32)[:, None], (SEP, W))
    pack = jnp.concatenate(
        [sep_inv[0, 0, 0].reshape(SEP * W, W), sep_up[0, 0, 0].reshape(SEP * W, W), parent_rows, jnp.zeros((8 - SEP, W), F32)],
        axis=0,
    )
    line = [along_x(pack, o) for o in range(1, NX)]
    codes_x = swap_x(codes)
    codes_below = along_y(codes, 1)
    codes_above = along_y(codes, -1)

    def wanted(these, direction):
        return jnp.where(these // table == direction, these % table, table)

    mid, products, acc = leaf_up(wanted(codes, 0), level.reshape(1), rhs_leaf, inv_leaf, blocks_leaf, rhs_sep)
    from_below = along_y(products, 1)
    from_above = along_y(products, -1)
    from_x = swap_x(products)

    bt, bn, gram, par, comp = blocks(my_x, pack, *line)
    others = [along_z(comp, o) for o in range(1, NZ)]
    ct, cn, cpar = chain_prep(others)

    idx = jnp.concatenate([wanted(codes_x, 1 + gx), wanted(codes_below, 4), wanted(codes_above, 3)])
    sums = collect(idx, acc, from_x, from_below, from_above)
    got = lax.all_to_all(sums, "leaf", 0, 0)

    piece = jax.ShapeDtypeStruct((NX * SEP, R // NX, W), F32)
    edge = jax.ShapeDtypeStruct((SEP, R // NX, W), F32)
    d, a = chain_call(gather_kernel, 0, "block_sum", (piece, edge), got, bt, par)
    a_all = spread(a, Z_GROUPS, NZ)
    zs, e = chain_call(up_kernel, 1, "block_up", (piece, edge), my_z, d, a_all, ct, cpar, bt, bn, gram, par)
    e_all = spread(e, Z_GROUPS, NZ)
    sol = chain_call(down_kernel, 1, "block_down", piece, my_z, zs, e_all, cn, cpar, bn, par)
    own = spread(sol)

    below = along_y(own, 1)
    above = along_y(own, -1)
    xs = swap_x(own)
    d_code = codes // table
    slot = jnp.where(d_code == 0, 0, jnp.where(d_code == 2 - gx, 1, jnp.where(d_code == 3, 2, 3)))
    outside = ((d_code == 1) & (gx == 0)) | ((d_code == 2) & (gx == lax.axis_size("gx") - 1))
    outside = outside | ((d_code == 3) & (gy == 0)) | ((d_code == 4) & (gy == lax.axis_size("gy") - 1))
    at = jnp.where(outside, 4 * table, slot * table + codes % table)
    leaf_sol = leaf_down(at, mid, inv_leaf, blocks_leaf, own, xs, below, above)
    mine = lax.dynamic_slice(own, (my_z[0] * NX, my_x[0] * SEP, 0, 0), (NX, SEP, R // NX, W))
    sep_sol = mine.transpose(1, 0, 2, 3).reshape(SEP, R, W)
    return (leaf_sol[None, None, None], sep_sol[None, None, None])


def solution(mesh):
    in_specs = (
        P("leaf", "gx", "gy", None, None, None),
        P("leaf", "gx", "gy", None, None, None),
        P("leaf", "gx", "gy", None, None, None, None),
        P("leaf", "gx", "gy", None, None),
        P("leaf", "gx", "gy", None, None, None),
        P("leaf", "gx", "gy", None, None, None),
        P("leaf", "gx", "gy", None, None, None),
        P("leaf", "gx", "gy", None),
    )
    out_specs = (P("leaf", "gx", "gy", None, None, None), P("leaf", "gx", "gy", None, None, None))
    return jax.shard_map(local, mesh=mesh, in_specs=in_specs, out_specs=out_specs, check_vma=False)
```

time: 1170 us -> 268 us (0.23)
  waiting for transfers between devices: 732 us -> 97.4 us
  starting transfers between devices: 234 us -> 61.2 us
  matrix products: 159 us -> 0 us
  Pallas kernels: 0 us -> 55 us
  blocking collectives: 0 us -> 41.5 us
  between operations: 14.3 us -> 0.9 us
    reduce_scatter x1 -> x0, waiting for transfers between devices: 219 us -> none  [local(): lax.psum_scatter(arriving, 'leaf', scatter_dimension=0, tiled=True)[0]]
    ppermute x70 -> x19, waiting for transfers between devices: 313 us -> 97.4 us  [the longest x6 37.6 us: along_y(): lax.ppermute(value, 'gy', [(i, i + offset) for i in range(count) if 0 <=...]
    all_gather x1 -> x0, waiting for transfers between devices: 200 us -> none  [local(): every_level = lax.all_gather(sep_sol[None], 'leaf', axis=0, tiled=True)]
    ppermute x70 -> x19, starting transfers between devices: 234 us -> 46.1 us  [the longest x7 19.8 us: along_z(): return lax.ppermute(value, 'leaf', pairs)]
    dot_general x196 -> x0, matrix products: 159 us -> none  [the longest x31 45.6 us: solve_up(): jnp.einsum('crw,cvw->crv', partial_mid, up_blocks, precision=HIGHEST)]
    pallas_call x0 -> x8, Pallas kernels: none -> 55 us  [the longest x1 15.5 us: leaf_down(): pl.pallas_call(leaf_down_kernel, grid_spec=spec, out_shape=jax.ShapeDtype...]
    all_to_all x0 -> x2, blocking collectives: none -> 41.5 us  [spread(): return lax.all_to_all(copies, 'leaf', 0, 0, axis_index_groups=groups)]
    all_to_all x0 -> x2, starting transfers between devices: none -> 15.1 us  [the longest x1 11.2 us: local(): got = lax.all_to_all(sums, 'leaf', 0, 0)]
  transfers between devices with their start and end apart: 72 -> 21, of which waited for: 70 -> 10; matrix products, arithmetic and copies ran while one was open for 0% -> 1% of each run, Pallas kernels for 0% -> 4%
where the time goes in v1:
time: 268 us; the launch traced here: 267 us
  waiting for transfers between devices  97.4 us (36%)
  starting transfers between devices  61.2 us (23%)
  Pallas kernels  55 us (21%)
  blocking collectives  41.5 us (15%)
  local copies, waits for them, and re-layouts  9.2 us (3%)
    all_to_all x2, blocking collectives, spread(): return lax.all_to_all(copies, 'leaf', 0, 0, axis_index_groups=groups)  41.5 us
    ppermute x6, waiting for transfers between devices, along_y(): lax.ppermute(value, 'gy', [(i, i + offset) for i in range(count) if 0 <=...  37.6 us
    ppermute x3, waiting for transfers between devices, along_x(): return lax.ppermute(value, 'leaf', pairs)  32.4 us
    ppermute x7, waiting for transfers between devices, along_z(): return lax.ppermute(value, 'leaf', pairs)  26.5 us
    ppermute x7, starting transfers between devices, along_z(): return lax.ppermute(value, 'leaf', pairs)  19.8 us
    pallas_call x1, Pallas kernels, leaf_down(): pl.pallas_call(leaf_down_kernel, grid_spec=spec, out_shape=jax.ShapeDtype...  15.5 us
    pallas_call x1, Pallas kernels, leaf_up(): pl.pallas_call(leaf_up_kernel, grid_spec=spec, out_shape=[jax.ShapeDtypeS...  14.6 us
    ppermute x6, starting transfers between devices, along_y(): lax.ppermute(value, 'gy', [(i, i + offset) for i in range(count) if 0 <=...  13.2 us
  transfers between devices with their start and end apart: 21, of which 10 were waited for; matrix products, arithmetic and copies ran while one was open for 1% of the time, Pallas kernels for 4%

profile of v1, /device:TPU:1, one launch (start us, length us, event | category | flops | bytes accessed | tf_op | source)
XLA Modules:
  0.0 266.9 jit_solution(10913712533830678521)
XLA Ops:
  2.0 14.6 %leaf_up.1 = (f32[48,16,128]{2,1,0:T(8,128)}, f32[96,16,128]{2,1,0:T(8,128)}, f32[129,16,128]{2,1,0:T(8,128)}) custom-call(s32[96]{0:T(128)} %get-tuple-element.32.idx_ref, s32[1]{0:T(128)} %bitcast.own_ref, f32[48,16,128]{2,1,0:T(8,128)} %bitcast.21, f32[48,128,128]{2,1,0:T(8,128)} %bitcast.19, f32[48,2,128,128]{3,2,1,0:T(8,128)} %bitcast.17, ...), custom_call_target="tpu_custom_call" | custom-call | flops 1000000000 | bytes 12000000 | tf_op jit(solution)/shard_map/leaf_up/pallas_call | solution.py:104
  16.6 3.3 %collective-permute-start.3 = (f32[96,16,128]{2,1,0:T(8,128)}, f32[96,16,128]{2,1,0:T(8,128)S(1)}, u32[]{:S(2)}, u32[]{:S(2)}) collective-permute-start(f32[96,16,128]{2,1,0:T(8,128)} %get-tuple-element.19), channel_id=1, source_target_pairs={{0,4},{4,0},{1,5},{5,1},{2,6},{6,2},{3,7},{7,3},{8,12},{12,8},{9,1... | collective-permute-start | bytes 2359304 | tf_op jit(solution)/shard_map/ppermute | solution.py:42
  24.0 4.6 %collective-permute-start.1 = (s32[96]{0:T(128)S(1)}, s32[96]{0:T(128)S(1)}, u32[]{:S(2)}, u32[]{:S(2)}) collective-permute-start(s32[96]{0:T(128)S(1)} %reshape_squeeze.9), channel_id=1, source_target_pairs={{0,1},{1,2},{2,3},{4,5},{5,6},{6,7},{8,9},{9,10},{10,11},{12,13},{... | collective-permute-start | bytes 1160 | tf_op jit(solution)/shard_map/ppermute | solution.py:38
  28.7 13.7 %collective-permute-done.2 = s32[96]{0:T(128)S(1)} collective-permute-done((s32[96]{0:T(128)S(1)}, s32[96]{0:T(128)S(1)}, u32[]{:S(2)}, u32[]{:S(2)}) %collective-permute-start.2) | collective-permute-done | bytes 416 | tf_op jit(solution)/shard_map/ppermute | solution.py:38
  46.5 4.8 %collect.1 = f32[32,16,4,128]{3,2,1,0:T(4,128)} custom-call(s32[288]{0:T(512)} %pad_add_fusion.idx_ref, f32[129,16,128]{2,1,0:T(8,128)} %get-tuple-element.18.acc_ref, f32[96,16,128]{2,1,0:T(8,128)} %copy-done.4, f32[96,16,128]{2,1,0:T(8,128)} %copy-done.5, f32[96,16,128]{2,1,0:T(8,128)} %copy-done.6), custom_call_target="tpu_custom_call" | custom-call | flops 1000000 | bytes 5000000 | tf_op jit(solution)/shard_map/collect/pallas_call | solution.py:150
  51.4 11.2 %all-to-all-start = ((f32[32,16,4,128]{3,2,1,0:T(4,128)}), f32[32,16,4,128]{3,2,1,0:T(4,128)S(1)}, u32[]{:S(2)}, u32[]{:S(2)}) async-start(f32[32,16,4,128]{3,2,1,0:T(4,128)} %collect.1), calls=%async_computation | async-start | bytes 2097152 | tf_op jit(solution)/shard_map/all_to_all | solution.py:430
  64.0 2.4 collective-permute-start.7
  67.6 17.9 %collective-permute-done.6.p1_ref = f32[1032,128]{1,0:T(8,128)S(1)} collective-permute-done((f32[1032,128]{1,0:T(8,128)S(1)}, f32[1032,128]{1,0:T(8,128)S(1)}, u32[]{:S(2)}, u32[]{:S(2)}) %collective-permute-start.6) | collective-permute-done | bytes 528416 | tf_op jit(solution)/shard_map/ppermute | solution.py:28
  85.5 14.5 %collective-permute-done.7.p2_ref = f32[1032,128]{1,0:T(8,128)S(1)} collective-permute-done((f32[1032,128]{1,0:T(8,128)S(1)}, f32[1032,128]{1,0:T(8,128)S(1)}, u32[]{:S(2)}, u32[]{:S(2)}) %collective-permute-start.7) | collective-permute-done | bytes 528416 | tf_op jit(solution)/shard_map/ppermute | solution.py:28
  100.8 5.0 %blocks.1 = (bf16[16,128,256]{2,1,0:T(8,128)(2,1)}, bf16[16,128,256]{2,1,0:T(8,128)(2,1)}, bf16[16,128,256]{2,1,0:T(8,128)(2,1)}, f32[4,8,128]{2,1,0:T(8,128)}, f32[520,128]{1,0:T(8,128)}) custom-call(s32[1]{0:T(128)} %bitcast.6.me_ref, f32[1032,128]{1,0:T(8,128)} %copy-done.7, f32[1032,128]{1,0:T(8,128)} %copy-done.18, f32[1032,128]{1,0:T(8,128)} %copy-done.19, ...), custom_call_target="tpu_custom_call" | custom-call | flops 1000000000 | bytes 5000000 | tf_op jit(solution)/shard_map/blocks/pallas_call | solution.py:210
  107.0 2.1 collective-permute-start.10
  109.1 2.2 collective-permute-start.11
  111.3 2.5 collective-permute-start.12
  113.8 2.0 collective-permute-start.13
  115.7 3.3 %collective-permute-start.14 = (f32[520,128]{1,0:T(8,128)}, f32[520,128]{1,0:T(8,128)S(1)}, u32[]{:S(2)}, u32[]{:S(2)}) collective-permute-start(f32[520,128]{1,0:T(8,128)} %get-tuple-element.24), channel_id=1, source_target_pairs={{0,192},{8,200},{16,208},{24,216},{32,224},{40,232},{48,240},{56,2... | collective-permute-start | bytes 798728 | tf_op jit(solution)/shard_map/ppermute | solution.py:33
  119.0 2.9 %collective-permute-done.10.refs_1_ = f32[520,128]{1,0:T(8,128)S(1)} collective-permute-done((f32[520,128]{1,0:T(8,128)}, f32[520,128]{1,0:T(8,128)S(1)}, u32[]{:S(2)}, u32[]{:S(2)}) %collective-permute-start.10) | collective-permute-done | bytes 266272 | tf_op jit(solution)/shard_map/ppermute | solution.py:33
  122.0 6.6 %collective-permute-start.15 = (f32[520,128]{1,0:T(8,128)}, f32[520,128]{1,0:T(8,128)S(1)}, u32[]{:S(2)}, u32[]{:S(2)}) collective-permute-start(f32[520,128]{1,0:T(8,128)} %get-tuple-element.24), channel_id=1, source_target_pairs={{0,224},{8,232},{16,240},{24,248},{32,0},{40,8},{48,16},{56,24},{6... | collective-permute-start | bytes 798728 | tf_op jit(solution)/shard_map/ppermute | solution.py:33
  129.6 2.8 %block_sum.1 = (f32[16,4,128]{2,1,0:T(4,128)}, f32[4,4,128]{2,1,0:T(4,128)}) custom-call(f32[32,16,4,128]{3,2,1,0:T(4,128)} %copy-done.1, bf16[16,128,256]{2,1,0:T(8,128)(2,1)} %get-tuple-element.20.bt_ref, f32[4,8,128]{2,1,0:T(8,128)} %get-tuple-element.21.par_ref), custom_call_target="tpu_custom_call" | custom-call | flops 100000000 | bytes 4000000 | tf_op jit(solution)/shard_map/block_sum/pallas_call | solution.py:328
  133.6 3.9 %all-to-all-start.1 = ((f32[8,4,4,128]{3,2,1,0:T(4,128)}), f32[8,4,4,128]{3,2,1,0:T(4,128)S(1)}, u32[]{:S(2)}, u32[]{:S(2)}) async-start(f32[8,4,4,128]{3,2,1,0:T(4,128)} %broadcast_in_dim.49), calls=%async_computation.1 | async-start | bytes 131072 | tf_op jit(solution)/shard_map/all_to_all | solution.py:390
  137.6 12.9 %collective-permute-done.12.refs_3_ = f32[520,128]{1,0:T(8,128)S(1)} collective-permute-done((f32[520,128]{1,0:T(8,128)}, f32[520,128]{1,0:T(8,128)S(1)}, u32[]{:S(2)}, u32[]{:S(2)}) %collective-permute-start.12) | collective-permute-done | bytes 266272 | tf_op jit(solution)/shard_map/ppermute | solution.py:33
  150.4 6.8 %collective-permute-done.14.refs_5_ = f32[520,128]{1,0:T(8,128)S(1)} collective-permute-done((f32[520,128]{1,0:T(8,128)}, f32[520,128]{1,0:T(8,128)S(1)}, u32[]{:S(2)}, u32[]{:S(2)}) %collective-permute-start.14) | collective-permute-done | bytes 266272 | tf_op jit(solution)/shard_map/ppermute | solution.py:33
  157.2 3.9 %collective-permute-done.15.refs_6_ = f32[520,128]{1,0:T(8,128)S(1)} collective-permute-done((f32[520,128]{1,0:T(8,128)}, f32[520,128]{1,0:T(8,128)S(1)}, u32[]{:S(2)}, u32[]{:S(2)}) %collective-permute-start.15) | collective-permute-done | bytes 266272 | tf_op jit(solution)/shard_map/ppermute | solution.py:33
  161.9 3.8 %chain_prep.1 = (bf16[32,128,256]{2,1,0:T(8,128)(2,1)}, bf16[32,128,256]{2,1,0:T(8,128)(2,1)}, f32[8,8,128]{2,1,0:T(8,128)}) custom-call(f32[520,128]{1,0:T(8,128)} %copy-done.8, f32[520,128]{1,0:T(8,128)} %copy-done.9, f32[520,128]{1,0:T(8,128)} %copy-done.10, f32[520,128]{1,0:T(8,128)} %copy-done.11, f32[520,128]{1,0:T(8,128)} %copy-done.12, ...), custom_call_target="tpu_custom_call" | custom-call | flops 1000000 | bytes 6000000 | tf_op jit(solution)/shard_map/chain_prep/pallas_call | solution.py:239
  166.3 4.3 %block_up.1 = (f32[16,4,128]{2,1,0:T(4,128)}, f32[4,4,128]{2,1,0:T(4,128)}) custom-call(s32[1]{0:T(128)} %bitcast.5.me_ref, f32[16,4,128]{2,1,0:T(4,128)} %get-tuple-element.22.d_ref, f32[8,4,4,128]{3,2,1,0:T(4,128)} %copy-done.15, bf16[32,128,256]{2,1,0:T(8,128)(2,1)} %get-tuple-element.25.ct_ref, f32[8,8,128]{2,1,0:T(8,128)} %get-tuple-element.26.cpar_ref, ...), custom_call_target="tpu_custom_call" | custom-call | flops 100000000 | bytes 4000000 | tf_op jit(solution)/shard_map/block_up/pallas_call | solution.py:328
  171.3 12.9 %all_to_all.20.all_ref = f32[8,4,4,128]{3,2,1,0:T(4,128)} all-to-all(f32[8,4,4,128]{3,2,1,0:T(4,128)S(1)} %broadcast_in_dim.50), channel_id=1, replica_groups={{0,32,64,96,128,160,192,224},{8,40,72,104,136,168,200,232},{16,48,80,11..., dimensions={0} | all-to-all | bytes 131072 | tf_op jit(solution)/shard_map/all_to_all | solution.py:390
  184.2 4.2 %block_down.1 = f32[16,4,128]{2,1,0:T(4,128)} custom-call(s32[1]{0:T(128)} %bitcast.5.me_ref, f32[16,4,128]{2,1,0:T(4,128)} %get-tuple-element.29.z_ref, f32[8,4,4,128]{3,2,1,0:T(4,128)} %all_to_all.20.all_ref, bf16[32,128,256]{2,1,0:T(8,128)(2,1)} %get-tuple-element.31.cn_ref, f32[8,8,128]{2,1,0:T(8,128)} %get-tuple-element.26.cpar_ref, ...), custom_call_target="tpu_custom_call" | custom-call | flops 100000000 | bytes 4000000 | tf_op jit(solution)/shard_map/block_down/pallas_call | solution.py:328
  189.4 28.6 %all_to_all.21.own_ref = f32[32,16,4,128]{3,2,1,0:T(4,128)S(1)} all-to-all(f32[32,16,4,128]{3,2,1,0:T(4,128)S(1)} %broadcast_in_dim.51), channel_id=1, replica_groups=mesh['leaf'=32,'gx'=2,'gy'=4] {'leaf'}, dimensions={0} | all-to-all | bytes 2097152 | tf_op jit(solution)/shard_map/all_to_all | solution.py:390
  218.0 3.7 %collective-permute-start.16 = (f32[32,16,4,128]{3,2,1,0:T(4,128)S(1)}, f32[32,16,4,128]{3,2,1,0:T(4,128)S(1)}, u32[]{:S(2)}, u32[]{:S(2)}) collective-permute-start(f32[32,16,4,128]{3,2,1,0:T(4,128)S(1)} %all_to_all.21.own_ref), channel_id=1, source_target_pairs={{0,4},{4,0},{1,5},{5,1},{2,6},{6,2},{3,7},{7,3},{8,12},{12,8},{9,1... | collective-permute-start | bytes 3145736 | tf_op jit(solution)/shard_map/ppermute | solution.py:42
  221.7 3.2 %collective-permute-start.17 = (f32[32,16,4,128]{3,2,1,0:T(4,128)S(1)}, f32[32,16,4,128]{3,2,1,0:T(4,128)S(1)}, u32[]{:S(2)}, u32[]{:S(2)}) collective-permute-start(f32[32,16,4,128]{3,2,1,0:T(4,128)S(1)} %all_to_all.21.own_ref), channel_id=1, source_target_pairs={{0,1},{1,2},{2,3},{4,5},{5,6},{6,7},{8,9},{9,10},{10,11},{12,13},{... | collective-permute-start | bytes 3145736 | tf_op jit(solution)/shard_map/ppermute | solution.py:38
  227.4 19.9 %collective-permute-done.17.ym_ref = f32[32,16,4,128]{3,2,1,0:T(4,128)S(1)} collective-permute-done((f32[32,16,4,128]{3,2,1,0:T(4,128)S(1)}, f32[32,16,4,128]{3,2,1,0:T(4,128)S(1)}, u32[]{:S(2)}, u32[]{:S(2)}) %collective-permute-start.17) | collective-permute-done | bytes 1048608 | tf_op jit(solution)/shard_map/ppermute | solution.py:38
  247.4 4.0 %collective-permute-done.18.yp_ref = f32[32,16,4,128]{3,2,1,0:T(4,128)} collective-permute-done((f32[32,16,4,128]{3,2,1,0:T(4,128)S(1)}, f32[32,16,4,128]{3,2,1,0:T(4,128)}, u32[]{:S(2)}, u32[]{:S(2)}) %collective-permute-start.18) | collective-permute-done | bytes 1048608 | tf_op jit(solution)/shard_map/ppermute | solution.py:38
  251.4 15.5 %leaf_down.1 = f32[48,16,128]{2,1,0:T(8,128)} custom-call(s32[96]{0:T(128)} %or_select_fusion.idx_ref, f32[48,16,128]{2,1,0:T(8,128)} %get-tuple-element.17.mid_ref, f32[48,128,128]{2,1,0:T(8,128)} %bitcast.20, f32[48,2,128,128]{3,2,1,0:T(8,128)} %bitcast.18, f32[32,16,4,128]{3,2,1,0:T(4,128)} %copy-done, f32[32,16,4,128]{3,2,1,0:T(4,128)} %copy-done.2, ...), custom_call_target="tpu_custom_call" | custom-call | flops 1000000000 | bytes 14000000 | tf_op jit(solution)/shard_map/leaf_down/pallas_call | solution.py:379
  (79 shorter events, 22.0 us)
Async XLA Ops:
  16.6 28.5 %collective-permute-start.3 = (f32[96,16,128]{2,1,0:T(8,128)}, f32[96,16,128]{2,1,0:T(8,128)S(1)}, u32[]{:S(2)}, u32[]{:S(2)}) collective-permute-start(f32[96,16,128]{2,1,0:T(8,128)} %get-tuple-element.19), channel_id=1, source_target_pairs={{0,4},{4,0},{1,5},{5,1},{2,6},{6,2},{3,7},{7,3},{8,12},{12,8},{9,1... | collective-permute-start | bytes 2359304 | tf_op jit(solution)/shard_map/ppermute | solution.py:42
  19.9 25.2 %collective-permute-start.4 = (f32[96,16,128]{2,1,0:T(8,128)}, f32[96,16,128]{2,1,0:T(8,128)S(1)}, u32[]{:S(2)}, u32[]{:S(2)}) collective-permute-start(f32[96,16,128]{2,1,0:T(8,128)} %get-tuple-element.19), channel_id=1, source_target_pairs={{0,1},{1,2},{2,3},{4,5},{5,6},{6,7},{8,9},{9,10},{10,11},{12,13},{... | collective-permute-start | bytes 2359304 | tf_op jit(solution)/shard_map/ppermute | solution.py:38
  21.4 23.7 %collective-permute-start.5 = (f32[96,16,128]{2,1,0:T(8,128)}, f32[96,16,128]{2,1,0:T(8,128)S(1)}, u32[]{:S(2)}, u32[]{:S(2)}) collective-permute-start(f32[96,16,128]{2,1,0:T(8,128)} %get-tuple-element.19), channel_id=1, source_target_pairs={{1,0},{2,1},{3,2},{5,4},{6,5},{7,6},{9,8},{10,9},{11,10},{13,12},{... | collective-permute-start | bytes 2359304 | tf_op jit(solution)/shard_map/ppermute | solution.py:38
  22.7 19.6 %collective-permute-start.2 = (s32[96]{0:T(128)S(1)}, s32[96]{0:T(128)S(1)}, u32[]{:S(2)}, u32[]{:S(2)}) collective-permute-start(s32[96]{0:T(128)S(1)} %reshape_squeeze.9), channel_id=1, source_target_pairs={{1,0},{2,1},{3,2},{5,4},{6,5},{7,6},{9,8},{10,9},{11,10},{13,12},{... | collective-permute-start | bytes 1160 | tf_op jit(solution)/shard_map/ppermute | solution.py:38
  24.0 19.6 %collective-permute-start.1 = (s32[96]{0:T(128)S(1)}, s32[96]{0:T(128)S(1)}, u32[]{:S(2)}, u32[]{:S(2)}) collective-permute-start(s32[96]{0:T(128)S(1)} %reshape_squeeze.9), channel_id=1, source_target_pairs={{0,1},{1,2},{2,3},{4,5},{5,6},{6,7},{8,9},{9,10},{10,11},{12,13},{... | collective-permute-start | bytes 1160 | tf_op jit(solution)/shard_map/ppermute | solution.py:38
  42.4 2.1 collective-permute-start
  51.4 11.2 %copy-start.20 = (s32[1,1,1,4]{3,2,1,0:T(1,128)S(1)}, s32[1,1,1,4]{3,2,1,0:T(1,128)}, u32[]{:S(2)}) copy-start(s32[1,1,1,4]{3,2,1,0:T(1,128)} %param.15) | copy-start | bytes 52
  51.4 11.3 %copy-start.16 = (f32[1,1,1,4,128,128]{5,4,3,2,1,0:T(8,128)S(1)}, f32[1,1,1,4,128,128]{5,4,3,2,1,0:T(8,128)}, u32[]{:S(2)}) copy-start(f32[1,1,1,4,128,128]{5,4,3,2,1,0:T(8,128)} %param.13) | copy-start | bytes 786436
  51.4 11.3 %copy-start.17 = (f32[1,1,1,4,128,128]{5,4,3,2,1,0:T(8,128)S(1)}, f32[1,1,1,4,128,128]{5,4,3,2,1,0:T(8,128)}, u32[]{:S(2)}) copy-start(f32[1,1,1,4,128,128]{5,4,3,2,1,0:T(8,128)} %param.14) | copy-start | bytes 786436
  51.4 77.2 %all-to-all-start = ((f32[32,16,4,128]{3,2,1,0:T(4,128)}), f32[32,16,4,128]{3,2,1,0:T(4,128)S(1)}, u32[]{:S(2)}, u32[]{:S(2)}) async-start(f32[32,16,4,128]{3,2,1,0:T(4,128)} %collect.1), calls=%async_computation | async-start | bytes 2097152 | tf_op jit(solution)/shard_map/all_to_all | solution.py:430
  62.7 37.3 %copy-start.7 = (f32[1032,128]{1,0:T(8,128)}, f32[1032,128]{1,0:T(8,128)S(1)}, u32[]{:S(2)}) copy-start(f32[1032,128]{1,0:T(8,128)S(1)} %concatenate.7.p0_ref) | copy-start | bytes 1585156
  62.7 22.8 %collective-permute-start.6 = (f32[1032,128]{1,0:T(8,128)S(1)}, f32[1032,128]{1,0:T(8,128)S(1)}, u32[]{:S(2)}, u32[]{:S(2)}) collective-permute-start(f32[1032,128]{1,0:T(8,128)S(1)} %concatenate.7.p0_ref), channel_id=1, source_target_pairs={{0,8},{8,16},{16,24},{24,0},{32,40},{40,48},{48,56},{56,32},{64,72... | collective-permute-start | bytes 1585160 | tf_op jit(solution)/shard_map/ppermute | solution.py:28
  64.0 36.0 %collective-permute-start.7 = (f32[1032,128]{1,0:T(8,128)S(1)}, f32[1032,128]{1,0:T(8,128)S(1)}, u32[]{:S(2)}, u32[]{:S(2)}) collective-permute-start(f32[1032,128]{1,0:T(8,128)S(1)} %concatenate.7.p0_ref), channel_id=1, source_target_pairs={{0,16},{8,24},{16,0},{24,8},{32,48},{40,56},{48,32},{56,40},{64,80... | collective-permute-start | bytes 1585160 | tf_op jit(solution)/shard_map/ppermute | solution.py:28
  66.4 33.6 %collective-permute-start.8 = (f32[1032,128]{1,0:T(8,128)S(1)}, f32[1032,128]{1,0:T(8,128)}, u32[]{:S(2)}, u32[]{:S(2)}) collective-permute-start(f32[1032,128]{1,0:T(8,128)S(1)} %concatenate.7.p0_ref), channel_id=1, source_target_pairs={{0,24},{8,0},{16,8},{24,16},{32,56},{40,32},{48,40},{56,48},{64,88... | collective-permute-start | bytes 1585160 | tf_op jit(solution)/shard_map/ppermute | solution.py:28
  85.5 14.5 %copy-start.18 = (f32[1032,128]{1,0:T(8,128)}, f32[1032,128]{1,0:T(8,128)S(1)}, u32[]{:S(2)}) copy-start(f32[1032,128]{1,0:T(8,128)S(1)} %collective-permute-done.6.p1_ref) | copy-start | bytes 1585156
  105.8 9.9 %collective-permute-start.9 = (f32[520,128]{1,0:T(8,128)}, f32[520,128]{1,0:T(8,128)S(1)}, u32[]{:S(2)}, u32[]{:S(2)}) collective-permute-start(f32[520,128]{1,0:T(8,128)} %get-tuple-element.24), channel_id=1, source_target_pairs={{0,32},{8,40},{16,48},{24,56},{32,64},{40,72},{48,80},{56,88},{64,... | collective-permute-start | bytes 798728 | tf_op jit(solution)/shard_map/ppermute | solution.py:33
  107.0 15.0 %collective-permute-start.10 = (f32[520,128]{1,0:T(8,128)}, f32[520,128]{1,0:T(8,128)S(1)}, u32[]{:S(2)}, u32[]{:S(2)}) collective-permute-start(f32[520,128]{1,0:T(8,128)} %get-tuple-element.24), channel_id=1, source_target_pairs={{0,64},{8,72},{16,80},{24,88},{32,96},{40,104},{48,112},{56,120},{... | collective-permute-start | bytes 798728 | tf_op jit(solution)/shard_map/ppermute | solution.py:33
  109.1 28.5 %collective-permute-start.11 = (f32[520,128]{1,0:T(8,128)}, f32[520,128]{1,0:T(8,128)S(1)}, u32[]{:S(2)}, u32[]{:S(2)}) collective-permute-start(f32[520,128]{1,0:T(8,128)} %get-tuple-element.24), channel_id=1, source_target_pairs={{0,96},{8,104},{16,112},{24,120},{32,128},{40,136},{48,144},{56,15... | collective-permute-start | bytes 798728 | tf_op jit(solution)/shard_map/ppermute | solution.py:33
  111.3 39.2 %collective-permute-start.12 = (f32[520,128]{1,0:T(8,128)}, f32[520,128]{1,0:T(8,128)S(1)}, u32[]{:S(2)}, u32[]{:S(2)}) collective-permute-start(f32[520,128]{1,0:T(8,128)} %get-tuple-element.24), channel_id=1, source_target_pairs={{0,128},{8,136},{16,144},{24,152},{32,160},{40,168},{48,176},{56,1... | collective-permute-start | bytes 798728 | tf_op jit(solution)/shard_map/ppermute | solution.py:33
  113.8 36.7 %collective-permute-start.13 = (f32[520,128]{1,0:T(8,128)}, f32[520,128]{1,0:T(8,128)S(1)}, u32[]{:S(2)}, u32[]{:S(2)}) collective-permute-start(f32[520,128]{1,0:T(8,128)} %get-tuple-element.24), channel_id=1, source_target_pairs={{0,160},{8,168},{16,176},{24,184},{32,192},{40,200},{48,208},{56,2... | collective-permute-start | bytes 798728 | tf_op jit(solution)/shard_map/ppermute | solution.py:33
  115.7 45.4 %copy-start.8 = (f32[520,128]{1,0:T(8,128)}, f32[520,128]{1,0:T(8,128)S(1)}, u32[]{:S(2)}) copy-start(f32[520,128]{1,0:T(8,128)S(1)} %collective-permute-done.9.refs_0_) | copy-start | bytes 798724
  115.7 41.5 %collective-permute-start.14 = (f32[520,128]{1,0:T(8,128)}, f32[520,128]{1,0:T(8,128)S(1)}, u32[]{:S(2)}, u32[]{:S(2)}) collective-permute-start(f32[520,128]{1,0:T(8,128)} %get-tuple-element.24), channel_id=1, source_target_pairs={{0,192},{8,200},{16,208},{24,216},{32,224},{40,232},{48,240},{56,2... | collective-permute-start | bytes 798728 | tf_op jit(solution)/shard_map/ppermute | solution.py:33
  122.0 39.1 %copy-start.9 = (f32[520,128]{1,0:T(8,128)}, f32[520,128]{1,0:T(8,128)S(1)}, u32[]{:S(2)}) copy-start(f32[520,128]{1,0:T(8,128)S(1)} %collective-permute-done.10.refs_1_) | copy-start | bytes 798724
  122.0 39.1 %collective-permute-start.15 = (f32[520,128]{1,0:T(8,128)}, f32[520,128]{1,0:T(8,128)S(1)}, u32[]{:S(2)}, u32[]{:S(2)}) collective-permute-start(f32[520,128]{1,0:T(8,128)} %get-tuple-element.24), channel_id=1, source_target_pairs={{0,224},{8,232},{16,240},{24,248},{32,0},{40,8},{48,16},{56,24},{6... | collective-permute-start | bytes 798728 | tf_op jit(solution)/shard_map/ppermute | solution.py:33
  133.6 32.0 %all-to-all-start.1 = ((f32[8,4,4,128]{3,2,1,0:T(4,128)}), f32[8,4,4,128]{3,2,1,0:T(4,128)S(1)}, u32[]{:S(2)}, u32[]{:S(2)}) async-start(f32[8,4,4,128]{3,2,1,0:T(4,128)} %broadcast_in_dim.49), calls=%async_computation.1 | async-start | bytes 131072 | tf_op jit(solution)/shard_map/all_to_all | solution.py:390
  137.6 23.6 %copy-start.10 = (f32[520,128]{1,0:T(8,128)}, f32[520,128]{1,0:T(8,128)S(1)}, u32[]{:S(2)}) copy-start(f32[520,128]{1,0:T(8,128)S(1)} %collective-permute-done.11.refs_2_) | copy-start | bytes 798724
  150.4 10.7 %copy-start.11 = (f32[520,128]{1,0:T(8,128)}, f32[520,128]{1,0:T(8,128)S(1)}, u32[]{:S(2)}) copy-start(f32[520,128]{1,0:T(8,128)S(1)} %collective-permute-done.12.refs_3_) | copy-start | bytes 798724
  218.0 33.4 %copy-start = (f32[32,16,4,128]{3,2,1,0:T(4,128)}, f32[32,16,4,128]{3,2,1,0:T(4,128)S(1)}, u32[]{:S(2)}) copy-start(f32[32,16,4,128]{3,2,1,0:T(4,128)S(1)} %all_to_all.21.own_ref) | copy-start | bytes 3145732
  218.0 9.4 %collective-permute-start.16 = (f32[32,16,4,128]{3,2,1,0:T(4,128)S(1)}, f32[32,16,4,128]{3,2,1,0:T(4,128)S(1)}, u32[]{:S(2)}, u32[]{:S(2)}) collective-permute-start(f32[32,16,4,128]{3,2,1,0:T(4,128)S(1)} %all_to_all.21.own_ref), channel_id=1, source_target_pairs={{0,4},{4,0},{1,5},{5,1},{2,6},{6,2},{3,7},{7,3},{8,12},{12,8},{9,1... | collective-permute-start | bytes 3145736 | tf_op jit(solution)/shard_map/ppermute | solution.py:42
  221.7 25.6 %collective-permute-start.17 = (f32[32,16,4,128]{3,2,1,0:T(4,128)S(1)}, f32[32,16,4,128]{3,2,1,0:T(4,128)S(1)}, u32[]{:S(2)}, u32[]{:S(2)}) collective-permute-start(f32[32,16,4,128]{3,2,1,0:T(4,128)S(1)} %all_to_all.21.own_ref), channel_id=1, source_target_pairs={{0,1},{1,2},{2,3},{4,5},{5,6},{6,7},{8,9},{9,10},{10,11},{12,13},{... | collective-permute-start | bytes 3145736 | tf_op jit(solution)/shard_map/ppermute | solution.py:38
  224.9 26.4 %collective-permute-start.18 = (f32[32,16,4,128]{3,2,1,0:T(4,128)S(1)}, f32[32,16,4,128]{3,2,1,0:T(4,128)}, u32[]{:S(2)}, u32[]{:S(2)}) collective-permute-start(f32[32,16,4,128]{3,2,1,0:T(4,128)S(1)} %all_to_all.21.own_ref), channel_id=1, source_target_pairs={{1,0},{2,1},{3,2},{5,4},{6,5},{7,6},{9,8},{10,9},{11,10},{13,12},{... | collective-permute-start | bytes 3145736 | tf_op jit(solution)/shard_map/ppermute | solution.py:38
  227.4 24.0 %copy-start.2 = (f32[32,16,4,128]{3,2,1,0:T(4,128)}, f32[32,16,4,128]{3,2,1,0:T(4,128)S(1)}, u32[]{:S(2)}) copy-start(f32[32,16,4,128]{3,2,1,0:T(4,128)S(1)} %collective-permute-done.16.xs_ref) | copy-start | bytes 3145732
  (10 other events, 25.2 us)

commit v2 on v1

v2 whole, which is shorter than its diff:
```python
import jax
import jax.numpy as jnp
from jax import lax
from jax.experimental import pallas as pl
from jax.experimental.pallas import tpu as pltpu
from jax.sharding import PartitionSpec as P


F32 = jnp.float32
BF16 = jnp.bfloat16
W = 128
R = 16
SEP = 4
NX = 4
NZ = 8
FRONT = NZ // 2
TABLE = NX * NZ * SEP
STEP = 8
NN = (((1,), (0,)), ((), ()))
NT = (((1,), (1,)), ((), ()))
TN = (((0,), (0,)), ((), ()))

Z_GROUPS = [[z * NX + x for z in range(NZ)] for x in range(NX)]


def along_x(value, offset):
    pairs = [(z * NX + x, z * NX + (x + offset) % NX) for z in range(NZ) for x in range(NX)]
    return lax.ppermute(value, "leaf", pairs)


def along_y(value, offset):
    count = lax.axis_size("gy")
    return lax.ppermute(value, "gy", [(i, i + offset) for i in range(count) if 0 <= i + offset < count])


def swap_x(value):
    return lax.ppermute(value, "gx", [(0, 1), (1, 0)])


def parts(value):
    high = value.astype(BF16).astype(F32)
    return high, value - high


def rows_of(value):
    return jnp.concatenate(parts(value), axis=0).astype(BF16)


def cols_of(value):
    return jnp.concatenate(parts(value), axis=1).astype(BF16)


def folded(out, rows):
    out = out[:, :W] + out[:, W:]
    return out[:rows] + out[rows:]


def times(left, dims, right):
    out = lax.dot_general(rows_of(left), right, dims, preferred_element_type=F32)
    return folded(out, left.shape[0])


def leaf_up_kernel(idx_ref, own_ref, rhs_ref, inv_ref, edge_ref, sep_ref, mid_ref, prod_ref, acc_ref):
    step = pl.program_id(0)

    @pl.when(step == 0)
    def _():
        acc_ref[...] = jnp.zeros_like(acc_ref)
        for s in range(SEP):
            acc_ref[own_ref[0] * SEP + s] = -sep_ref[s]

    for s in range(STEP):
        mid = times(rhs_ref[s], NT, rows_of(inv_ref[s]))
        mid_ref[s] = mid
        for j in range(2):
            product = times(mid, NT, rows_of(edge_ref[s, j]))
            prod_ref[2 * s + j] = product
            at = idx_ref[(step * STEP + s) * 2 + j]
            acc_ref[at] += product


def leaf_up(idx, own, rhs, inv, edges, sep_rhs):
    count = rhs.shape[0]
    spec = pltpu.PrefetchScalarGridSpec(
        num_scalar_prefetch=2,
        grid=(count // STEP,),
        in_specs=[
            pl.BlockSpec((STEP, R, W), lambda i, *_: (i, 0, 0)),
            pl.BlockSpec((STEP, W, W), lambda i, *_: (i, 0, 0)),
            pl.BlockSpec((STEP, 2, W, W), lambda i, *_: (i, 0, 0, 0)),
            pl.BlockSpec((SEP, R, W), lambda i, *_: (0, 0, 0)),
        ],
        out_specs=[
            pl.BlockSpec((STEP, R, W), lambda i, *_: (i, 0, 0)),
            pl.BlockSpec((2 * STEP, R, W), lambda i, *_: (i, 0, 0)),
            pl.BlockSpec((NX * NZ * SEP + 1, R, W), lambda i, *_: (0, 0, 0)),
        ],
    )
    return pl.pallas_call(
        leaf_up_kernel,
        grid_spec=spec,
        out_shape=[
            jax.ShapeDtypeStruct((count, R, W), F32),
            jax.ShapeDtypeStruct((2 * count, R, W), F32),
            jax.ShapeDtypeStruct((NX * NZ * SEP + 1, R, W), F32),
        ],
        cost_estimate=pl.CostEstimate(flops=10**9, bytes_accessed=12 * 10**6, transcendentals=0),
        name="leaf_up",
    )(idx, own, rhs, inv, edges, sep_rhs)


def add_list(idx_ref, first, sums, list_ref):
    def add(i, carry):
        for m in range(8):
            n = i * 8 + m
            sums[idx_ref[first + n]] += list_ref[n]
        return carry

    lax.fori_loop(0, list_ref.shape[0] // 8, add, 0)


def collect_x_kernel(idx_ref, acc_ref, a_ref, sums_ref):
    sums_ref[...] = acc_ref[...]
    add_list(idx_ref, 0, sums_ref, a_ref)


def collect_kernel(idx_ref, acc_ref, b_ref, c_ref, out_ref, sums):
    sums[...] = acc_ref[...]
    add_list(idx_ref, 0, sums, b_ref)
    add_list(idx_ref, b_ref.shape[0], sums, c_ref)

    def place(z, carry):
        for k in range(NX * SEP):
            tile = sums[z * NX * SEP + k]
            for x in range(NX):
                out_ref[z * NX + x, k] = tile[4 * x : 4 * x + 4]
        return carry

    lax.fori_loop(0, NZ, place, 0)


def vmem():
    return pl.BlockSpec(memory_space=pltpu.VMEM)


def smem():
    return pl.BlockSpec(memory_space=pltpu.SMEM)


def collect_x(idx, acc, a):
    return pl.pallas_call(
        collect_x_kernel,
        in_specs=[smem(), vmem(), vmem()],
        out_specs=vmem(),
        out_shape=jax.ShapeDtypeStruct(acc.shape, F32),
        cost_estimate=pl.CostEstimate(flops=10**6, bytes_accessed=3 * 10**6, transcendentals=0),
        name="collect_x",
    )(idx, acc, a)


def collect(idx, acc, b, c):
    return pl.pallas_call(
        collect_kernel,
        in_specs=[smem()] + [vmem()] * 3,
        out_specs=vmem(),
        out_shape=jax.ShapeDtypeStruct((NX * NZ, NX * SEP, R // NX, W), F32),
        scratch_shapes=[pltpu.VMEM(acc.shape, F32)],
        cost_estimate=pl.CostEstimate(flops=10**6, bytes_accessed=5 * 10**6, transcendentals=0),
        name="collect",
    )(idx, acc, b, c)


def picked(rows, c, p):
    return rows[c : c + 1, :] == float(p)


def pack_kernel(inv_ref, up_ref, parent_ref, out_ref, gram_ref):
    for c in range(SEP):
        inv_cols = cols_of(inv_ref[c])
        out_ref[c * W : (c + 1) * W] = times(up_ref[c], NN, inv_cols)
        gram = lax.dot_general(inv_cols, inv_cols, TN, preferred_element_type=F32)
        gram_ref[c * W : (c + 1) * W] = folded(gram, W)
    rows = lax.broadcasted_iota(jnp.int32, (8, W), 0)
    parents = jnp.zeros((8, W), F32)
    for c in range(SEP):
        parents = jnp.where(rows == c, parent_ref[c].astype(F32), parents)
    out_ref[SEP * W : SEP * W + 8] = parents


def pack_own(inv, up, parent):
    return pl.pallas_call(
        pack_kernel,
        in_specs=[vmem(), vmem(), smem()],
        out_specs=[vmem()] * 2,
        out_shape=[jax.ShapeDtypeStruct((SEP * W + 8, W), F32), jax.ShapeDtypeStruct((SEP * W, W), F32)],
        cost_estimate=pl.CostEstimate(flops=10**8, bytes_accessed=10**6, transcendentals=0),
        name="pack",
    )(inv, up, parent)


def blocks_kernel(me_ref, p0_ref, p1_ref, p2_ref, p3_ref, bt_ref, bn_ref, par_ref, comp_ref, whole):
    me = me_ref[0]
    for o, ref in enumerate((p0_ref, p1_ref, p2_ref, p3_ref)):
        level = lax.rem(me - o + NX, NX)
        for c in range(SEP):
            mat = ref[c * W : (c + 1) * W]
            bn_ref[level * SEP + c] = cols_of(mat)
            bt_ref[level * SEP + c] = cols_of(mat.T)
        par_ref[level] = ref[SEP * W :]

    def joined(c):
        pair = bn_ref[c].astype(F32)
        return pair[:, :W] + pair[:, W:]

    comp = [joined(c) for c in range(SEP)]
    to = par_ref[0]
    for j in range(1, NX):
        mats = [joined(j * SEP + p) for p in range(SEP)]
        own = par_ref[j]
        following = []
        for c in range(SEP):
            mat = mats[SEP - 1]
            row = own[SEP - 1 : SEP]
            for p in range(SEP - 1):
                mat = jnp.where(picked(to, c, p), mats[p], mat)
                row = jnp.where(picked(to, c, p), own[p : p + 1], row)
            comp[c] = times(mat, NN, cols_of(comp[c]))
            following.append(row)
        to = jnp.concatenate(following + [own[SEP:]], axis=0)
    for c in range(SEP):
        whole[c] = comp[c]
    for n in range(NZ):
        comp_ref[n, :W] = whole[me]
        comp_ref[n, W:] = to


def blocks(me, *line):
    n = NX * SEP
    return pl.pallas_call(
        blocks_kernel,
        in_specs=[smem()] + [vmem()] * len(line),
        out_specs=[vmem()] * 4,
        out_shape=[
            jax.ShapeDtypeStruct((n, W, 2 * W), BF16),
            jax.ShapeDtypeStruct((n, W, 2 * W), BF16),
            jax.ShapeDtypeStruct((NX, 8, W), F32),
            jax.ShapeDtypeStruct((NZ, W + 8, W), F32),
        ],
        scratch_shapes=[pltpu.VMEM((SEP, W, W), F32)],
        cost_estimate=pl.CostEstimate(flops=10**9, bytes_accessed=5 * 10**6, transcendentals=0),
        name="blocks",
    )(me, *line)


def chain_prep_kernel(me_ref, m0_ref, m1_ref, m3_ref, m2a_ref, m2b_ref, *refs):
    grams, (ct_ref, cn_ref, par_ref, g_ref) = refs[:NX], refs[NX:]
    me = me_ref[0]
    for i, sources in enumerate(((m0_ref,), (m1_ref,), (m2a_ref, m2b_ref), (m3_ref,))):
        c = lax.rem(me - i + NX, NX)
        for b in range(NZ):
            ref, at = sources[0], b
            if len(sources) > 1 and at >= FRONT:
                ref, at = sources[1], at - FRONT
            mat = ref[at, :W]
            cn_ref[b * SEP + c] = cols_of(mat)
            ct_ref[b * SEP + c] = cols_of(mat.T)
        for k in range(SEP):
            g_ref[c * SEP + k] = cols_of(grams[i][k * W : (k + 1) * W])
    for b in range(NZ):
        par_ref[b] = m0_ref[b, W:]


def chain_prep(me, *line):
    n = NZ * SEP
    return pl.pallas_call(
        chain_prep_kernel,
        in_specs=[smem()] + [vmem()] * len(line),
        out_specs=[vmem()] * 4,
        out_shape=[
            jax.ShapeDtypeStruct((n, W, 2 * W), BF16),
            jax.ShapeDtypeStruct((n, W, 2 * W), BF16),
            jax.ShapeDtypeStruct((NZ, 8, W), F32),
            jax.ShapeDtypeStruct((NX * SEP, W, 2 * W), BF16),
        ],
        cost_estimate=pl.CostEstimate(flops=10**6, bytes_accessed=6 * 10**6, transcendentals=0),
        name="chain_prep",
    )(me, *line)


def lift(values, mats, base, parents):
    lifted = [times(values[c], NN, mats[base + c]) for c in range(SEP)]
    sums = []
    for p in range(SEP):
        total = jnp.where(picked(parents, 0, p), lifted[0], 0.0)
        for c in range(1, SEP):
            total = total + jnp.where(picked(parents, c, p), lifted[c], 0.0)
        sums.append(total)
    return sums


def lower(values, mats, base, parents):
    out = []
    for c in range(SEP):
        mine = values[SEP - 1]
        for p in range(SEP - 1):
            mine = jnp.where(picked(parents, c, p), values[p], mine)
        out.append(times(mine, NN, mats[base + c]))
    return out


def gather_kernel(got_ref, bt_ref, par_ref, d_ref, a_ref):
    d = got_ref[0]
    for n in range(1, NX * NZ):
        d = d + got_ref[n]
    d_ref[...] = -d
    incoming = [jnp.zeros((R // NX, W), F32)] * SEP
    for j in range(NX):
        values = [d_ref[j * SEP + c] - incoming[c] for c in range(SEP)]
        incoming = lift(values, bt_ref, j * SEP, par_ref[j])
    for c in range(SEP):
        for n in range(NZ):
            a_ref[n, c] = incoming[c]


def up_kernel(me_ref, d_ref, all_ref, ct_ref, cpar_ref, bt_ref, bn_ref, g_ref, par_ref, z_ref, e_ref):
    me = me_ref[0]

    def follow(b, incoming):
        moved = lift(incoming, ct_ref, b * SEP, cpar_ref[b])
        return [all_ref[b, c] + moved[c] for c in range(SEP)]

    incoming = lax.fori_loop(0, me, follow, [jnp.zeros((R // NX, W), F32)] * SEP)
    for j in range(NX):
        values = [d_ref[j * SEP + c] - incoming[c] for c in range(SEP)]
        for c in range(SEP):
            z_ref[j * SEP + c] = times(values[c], NN, g_ref[j * SEP + c])
        if j < NX - 1:
            incoming = lift(values, bt_ref, j * SEP, par_ref[j])
    above = [z_ref[(NX - 1) * SEP + c] for c in range(SEP)]
    for j in range(NX - 2, -1, -1):
        pushed = lower(above, bn_ref, j * SEP, par_ref[j])
        above = [z_ref[j * SEP + c] - pushed[c] for c in range(SEP)]
    for c in range(SEP):
        for n in range(NZ):
            e_ref[n, c] = above[c]


def down_kernel(me_ref, z_ref, all_ref, cn_ref, cpar_ref, bn_ref, par_ref, sol_ref):
    me = me_ref[0]

    def follow(i, above):
        b = NZ - 1 - i
        moved = lower(above, cn_ref, b * SEP, cpar_ref[b])
        return [all_ref[b, c] + moved[c] for c in range(SEP)]

    above = lax.fori_loop(0, NZ - 1 - me, follow, [jnp.zeros((R // NX, W), F32)] * SEP)
    for j in range(NX - 1, -1, -1):
        pushed = lower(above, bn_ref, j * SEP, par_ref[j])
        above = [z_ref[j * SEP + c] - pushed[c] for c in range(SEP)]
        for c in range(SEP):
            for n in range(NX * NZ):
                sol_ref[n, j * SEP + c] = above[c]


def chain_call(kernel, scalars, out_shape, *args):
    return pl.pallas_call(
        kernel,
        in_specs=[smem()] * scalars + [vmem()] * (len(args) - scalars),
        out_specs=jax.tree.map(lambda _: vmem(), out_shape),
        out_shape=out_shape,
        cost_estimate=pl.CostEstimate(flops=10**8, bytes_accessed=4 * 10**6, transcendentals=0),
    )(*args)


def pick_kernel(idx_ref, own_ref, *out_refs):
    count = out_refs[0].shape[0]

    def pick(i, carry):
        for m in range(8):
            n = i * 8 + m
            for k, out_ref in enumerate(out_refs):
                at = idx_ref[k * count + n]
                z, slot = at // (NX * SEP), at % (NX * SEP)
                tile = jnp.concatenate([own_ref[z * NX + x, slot] for x in range(NX)], axis=0)
                out_ref[n] = tile
        return carry

    lax.fori_loop(0, count // 8, pick, 0)


def pick(idx, own, lists):
    count = idx.shape[0] // lists
    return pl.pallas_call(
        pick_kernel,
        in_specs=[smem(), vmem()],
        out_specs=[vmem()] * lists,
        out_shape=[jax.ShapeDtypeStruct((count, R, W), F32)] * lists,
        cost_estimate=pl.CostEstimate(flops=10**6, bytes_accessed=3 * 10**6, transcendentals=0),
        name="pick",
    )(idx, own)


def leaf_down_kernel(slot_ref, mid_ref, inv_ref, edge_ref, *refs):
    lists, out_ref = refs[:-1], refs[-1]
    step = pl.program_id(0)

    def reached(s, j):
        slot = slot_ref[(step * STEP + s) * 2 + j]
        value = jnp.zeros((R, W), F32)
        for n, ref in enumerate(lists):
            value = jnp.where(slot == n, ref[2 * s + j], value)
        return value

    for s in range(STEP):
        pulled = times(reached(s, 0), NN, cols_of(edge_ref[s, 0]))
        pulled = pulled + times(reached(s, 1), NN, cols_of(edge_ref[s, 1]))
        out_ref[s] = times(mid_ref[s] - pulled, NN, cols_of(inv_ref[s]))


def leaf_down(slot, mid, inv, edges, *lists):
    count = mid.shape[0]
    spec = pltpu.PrefetchScalarGridSpec(
        num_scalar_prefetch=1,
        grid=(count // STEP,),
        in_specs=[
            pl.BlockSpec((STEP, R, W), lambda i, *_: (i, 0, 0)),
            pl.BlockSpec((STEP, W, W), lambda i, *_: (i, 0, 0)),
            pl.BlockSpec((STEP, 2, W, W), lambda i, *_: (i, 0, 0, 0)),
        ]
        + [pl.BlockSpec((2 * STEP, R, W), lambda i, *_: (i, 0, 0))] * len(lists),
        out_specs=pl.BlockSpec((STEP, R, W), lambda i, *_: (i, 0, 0)),
    )
    return pl.pallas_call(
        leaf_down_kernel,
        grid_spec=spec,
        out_shape=jax.ShapeDtypeStruct((count, R, W), F32),
        cost_estimate=pl.CostEstimate(flops=10**9, bytes_accessed=14 * 10**6, transcendentals=0),
        name="leaf_down",
    )(slot, mid, inv, edges, *lists)


def exchange(value, groups=None):
    return lax.all_to_all(value, "leaf", 0, 0, axis_index_groups=groups)


def local(leaf_rhs, leaf_inv, edge_blocks, edge_target, sep_rhs, sep_inv, sep_up, sep_parent):
    rhs_leaf = leaf_rhs[0, 0, 0]
    inv_leaf = leaf_inv[0, 0, 0]
    blocks_leaf = edge_blocks[0, 0, 0]
    codes = edge_target[0, 0, 0].reshape(-1)
    rhs_sep = sep_rhs[0, 0, 0]
    level = lax.axis_index("leaf").astype(jnp.int32)
    my_x = lax.rem(level, NX).reshape(1)
    my_z = lax.div(level, NX).reshape(1)
    gx = lax.axis_index("gx").astype(jnp.int32)
    gy = lax.axis_index("gy").astype(jnp.int32)

    own_pack, own_gram = pack_own(sep_inv[0, 0, 0], sep_up[0, 0, 0], sep_parent[0, 0, 0])
    line = [along_x(own_pack, o) for o in range(1, NX)]
    codes_x = swap_x(codes)
    codes_below = along_y(codes, 1)
    codes_above = along_y(codes, -1)

    def wanted(these, direction):
        return jnp.where(these // TABLE == direction, these % TABLE, TABLE)

    mid, products, acc = leaf_up(wanted(codes, 0), level.reshape(1), rhs_leaf, inv_leaf, blocks_leaf, rhs_sep)
    from_below = along_y(products, 1)
    from_above = along_y(products, -1)
    from_x = swap_x(products)

    grams = [own_gram] + [along_x(own_gram, o) for o in range(1, NX)]
    bt, bn, par, comp = blocks(my_x, own_pack, *line)
    columns = exchange(comp, Z_GROUPS)
    before = along_x(columns, 1)
    after = along_x(columns, -1)
    front = along_x(before[:FRONT], 1)
    back = along_x(after[FRONT:], -1)
    ct, cn, cpar, gram = chain_prep(my_x, columns, before, after, front, back, *grams)

    idx_x = wanted(codes_x, 1 + gx)
    idx_y = jnp.concatenate([wanted(codes_below, 4), wanted(codes_above, 3)])
    acc = collect_x(idx_x, acc, from_x)
    sums = collect(idx_y, acc, from_below, from_above)
    got = exchange(sums)

    piece = jax.ShapeDtypeStruct((NX * SEP, R // NX, W), F32)
    copies = jax.ShapeDtypeStruct((NZ, SEP, R // NX, W), F32)
    d, a = chain_call(gather_kernel, 0, (piece, copies), got, bt, par)
    a_all = exchange(a, Z_GROUPS)
    zs, e = chain_call(up_kernel, 1, (piece, copies), my_z, d, a_all, ct, cpar, bt, bn, gram, par)
    e_all = exchange(e, Z_GROUPS)
    sol = jax.ShapeDtypeStruct((NX * NZ, NX * SEP, R // NX, W), F32)
    sol = chain_call(down_kernel, 1, sol, my_z, zs, e_all, cn, cpar, bn, par)
    own = exchange(sol)

    to_below, to_above = pick(jnp.concatenate([idx_y[: codes.size], idx_y[codes.size :]]) % TABLE, own, 2)
    from_above = along_y(to_below, -1)
    from_below = along_y(to_above, 1)
    to_x, mine_list = pick(jnp.concatenate([idx_x, codes]) % TABLE, own, 2)
    from_x = swap_x(to_x)
    d_code = codes // TABLE
    slot = jnp.where(d_code == 0, 0, jnp.where(d_code == 2 - gx, 1, jnp.where(d_code == 3, 2, 3)))
    outside = ((d_code == 1) & (gx == 0)) | ((d_code == 2) & (gx == lax.axis_size("gx") - 1))
    outside = outside | ((d_code == 3) & (gy == 0)) | ((d_code == 4) & (gy == lax.axis_size("gy") - 1))
    slot = jnp.where(outside, 4, slot)
    leaf_sol = leaf_down(slot, mid, inv_leaf, blocks_leaf, mine_list, from_x, from_below, from_above)
    mine = lax.dynamic_slice(own, (my_z[0] * NX, my_x[0] * SEP, 0, 0), (NX, SEP, R // NX, W))
    sep_sol = mine.transpose(1, 0, 2, 3).reshape(SEP, R, W)
    return (leaf_sol[None, None, None], sep_sol[None, None, None])


def solution(mesh):
    in_specs = (
        P("leaf", "gx", "gy", None, None, None),
        P("leaf", "gx", "gy", None, None, None),
        P("leaf", "gx", "gy", None, None, None, None),
        P("leaf", "gx", "gy", None, None),
        P("leaf", "gx", "gy", None, None, None),
        P("leaf", "gx", "gy", None, None, None),
        P("leaf", "gx", "gy", None, None, None),
        P("leaf", "gx", "gy", None),
    )
    out_specs = (P("leaf", "gx", "gy", None, None, None), P("leaf", "gx", "gy", None, None, None))
    return jax.shard_map(local, mesh=mesh, in_specs=in_specs, out_specs=out_specs, check_vma=False)
```

time: 268 us -> 247 us (0.922)
  blocking collectives: 41.5 us -> 15 us
  waiting for transfers between devices: 97.4 us -> 90.2 us
  starting transfers between devices: 61.2 us -> 66.9 us
  Pallas kernels: 55 us -> 59.9 us
    all_to_all x2 -> x1, blocking collectives: 41.5 us -> 15 us  [exchange(): return lax.all_to_all(value, 'leaf', 0, 0, axis_index_groups=groups)]
    ppermute x7 -> x0, waiting for transfers between devices: 26.5 us -> none  [along_z(): return lax.ppermute(value, 'leaf', pairs)]
    all_to_all x2 -> x4, waiting for transfers between devices: 0.01 us -> 21.5 us  [exchange(): return lax.all_to_all(value, 'leaf', 0, 0, axis_index_groups=groups)]
    ppermute x7 -> x0, starting transfers between devices: 19.8 us -> none  [along_z(): return lax.ppermute(value, 'leaf', pairs)]
    all_to_all x2 -> x4, starting transfers between devices: 15.1 us -> 28.9 us  [exchange(): return lax.all_to_all(value, 'leaf', 0, 0, axis_index_groups=groups)]
    pallas_call x3 -> x7, Pallas kernels: 13.7 us -> 24.9 us  [the longest x2 7.49 us: pick(): pl.pallas_call(pick_kernel, in_specs=[smem(), vmem()], out_specs=[vmem()]...]
    ppermute x3 -> x10, starting transfers between devices: 4.88 us -> 15.5 us  [along_x(): return lax.ppermute(value, 'leaf', pairs)]
    pallas_call x1, Pallas kernels: 15.5 us -> 11.1 us  [leaf_down(): pl.pallas_call(leaf_down_kernel, grid_spec=spec, out_shape=jax.ShapeDtype...]
  transfers between devices with their start and end apart: 21 -> 23, of which waited for: 10 -> 10; matrix products, arithmetic and copies ran while one was open for 1% -> 2% of each run, Pallas kernels for 4% -> 12%
where the time goes in v2:
time: 247 us; the launch traced here: 245 us
  waiting for transfers between devices  90.2 us (37%)
  starting transfers between devices  66.9 us (27%)
  Pallas kernels  59.9 us (24%)
  blocking collectives  15 us (6%)
  local copies, waits for them, and re-layouts  9.41 us (4%)
  other arithmetic  3 us (1%)
    ppermute x6, waiting for transfers between devices, along_y(): lax.ppermute(value, 'gy', [(i, i + offset) for i in range(count) if 0 <=...  36.2 us
    ppermute x10, waiting for transfers between devices, along_x(): return lax.ppermute(value, 'leaf', pairs)  32.5 us
    all_to_all x4, starting transfers between devices, exchange(): return lax.all_to_all(value, 'leaf', 0, 0, axis_index_groups=groups)  28.9 us
    all_to_all x4, waiting for transfers between devices, exchange(): return lax.all_to_all(value, 'leaf', 0, 0, axis_index_groups=groups)  21.5 us
    ppermute x10, starting transfers between devices, along_x(): return lax.ppermute(value, 'leaf', pairs)  15.5 us
    all_to_all x1, blocking collectives, exchange(): return lax.all_to_all(value, 'leaf', 0, 0, axis_index_groups=groups)  15 us
    ppermute x6, starting transfers between devices, along_y(): lax.ppermute(value, 'gy', [(i, i + offset) for i in range(count) if 0 <=...  13.3 us
    pallas_call x1, Pallas kernels, leaf_up(): pl.pallas_call(leaf_up_kernel, grid_spec=spec, out_shape=[jax.ShapeDtypeS...  12.1 us
  transfers between devices with their start and end apart: 23, of which 10 were waited for; matrix products, arithmetic and copies ran while one was open for 2% of the time, Pallas kernels for 12%

profile of v2, /device:TPU:1, one launch (start us, length us, event | category | flops | bytes accessed | tf_op | source)
XLA Modules:
  0.0 245.3 jit_solution(434896327883294655)
XLA Ops:
  0.6 2.2 pack.1
  2.9 2.0 collective-permute-start.6
  4.9 2.4 collective-permute-start.7
  10.2 8.9 %collective-permute-done.7.p2_ref = f32[520,128]{1,0:T(8,128)S(1)} collective-permute-done((f32[520,128]{1,0:T(8,128)}, f32[520,128]{1,0:T(8,128)S(1)}, u32[]{:S(2)}, u32[]{:S(2)}) %collective-permute-start.7) | collective-permute-done | bytes 266272 | tf_op jit(solution)/shard_map/ppermute | solution.py:28
  19.9 3.3 %blocks.1 = (bf16[16,128,256]{2,1,0:T(8,128)(2,1)}, bf16[16,128,256]{2,1,0:T(8,128)(2,1)}, f32[4,8,128]{2,1,0:T(8,128)}, f32[8,136,128]{2,1,0:T(8,128)}) custom-call(s32[1]{0:T(128)} %bitcast.6.me_ref, f32[520,128]{1,0:T(8,128)} %get-tuple-element.26.p0_ref, f32[520,128]{1,0:T(8,128)} %copy-done.17, f32[520,128]{1,0:T(8,128)} %copy-done.18, ...), custom_call_target="tpu_custom_call" | custom-call | flops 1000000000 | bytes 5000000 | tf_op jit(solution)/shard_map/blocks/pallas_call | solution.py:239
  23.3 8.2 %all-to-all-start.2 = ((f32[8,136,128]{2,1,0:T(8,128)}), f32[8,136,128]{2,1,0:T(8,128)S(1)}, u32[]{:S(2)}, u32[]{:S(2)}) async-start(f32[8,136,128]{2,1,0:T(8,128)} %get-tuple-element.31), calls=%async_computation.2 | async-start | bytes 1114112 | tf_op jit(solution)/shard_map/all_to_all | solution.py:443
  32.0 12.1 %leaf_up.1 = (f32[48,16,128]{2,1,0:T(8,128)}, f32[96,16,128]{2,1,0:T(8,128)}, f32[129,16,128]{2,1,0:T(8,128)}) custom-call(s32[96]{0:T(128)} %get-tuple-element.44.idx_ref, s32[1]{0:T(128)} %bitcast.own_ref, f32[48,16,128]{2,1,0:T(8,128)} %bitcast.20, f32[48,128,128]{2,1,0:T(8,128)} %bitcast.18, f32[48,2,128,128]{3,2,1,0:T(8,128)} %bitcast.16, ...), custom_call_target="tpu_custom_call" | custom-call | flops 1000000000 | bytes 12000000 | tf_op jit(solution)/shard_map/leaf_up/pallas_call | solution.py:99
  46.0 3.2 %collective-permute-start.4 = (f32[96,16,128]{2,1,0:T(8,128)}, f32[96,16,128]{2,1,0:T(8,128)S(1)}, u32[]{:S(2)}, u32[]{:S(2)}) collective-permute-start(f32[96,16,128]{2,1,0:T(8,128)} %get-tuple-element.25), channel_id=1, source_target_pairs={{0,1},{1,2},{2,3},{4,5},{5,6},{6,7},{8,9},{9,10},{10,11},{12,13},{... | collective-permute-start | bytes 2359304 | tf_op jit(solution)/shard_map/ppermute | solution.py:33
  52.2 17.9 %collective-permute-done.2 = s32[96]{0:T(128)S(1)} collective-permute-done((s32[96]{0:T(128)S(1)}, s32[96]{0:T(128)S(1)}, u32[]{:S(2)}, u32[]{:S(2)}) %collective-permute-start.2) | collective-permute-done | bytes 416 | tf_op jit(solution)/shard_map/ppermute | solution.py:33
  70.1 3.1 %collective-permute-start.1 = (s32[96]{0:T(128)S(1)}, s32[96]{0:T(128)S(1)}, u32[]{:S(2)}, u32[]{:S(2)}) collective-permute-start(s32[96]{0:T(128)S(1)} %reshape_squeeze.3), channel_id=1, source_target_pairs={{0,1},{1,2},{2,3},{4,5},{5,6},{6,7},{8,9},{9,10},{10,11},{12,13},{... | collective-permute-start | bytes 1160 | tf_op jit(solution)/shard_map/ppermute | solution.py:33
  76.1 3.1 %collect_x.1.acc_ref = f32[129,16,128]{2,1,0:T(8,128)} custom-call(s32[96]{0:T(128)} %compare_select_fusion.6.idx_ref, f32[129,16,128]{2,1,0:T(8,128)} %get-tuple-element.24.acc_ref, f32[96,16,128]{2,1,0:T(8,128)} %copy-done.7), custom_call_target="tpu_custom_call" | custom-call | flops 1000000 | bytes 3000000 | tf_op jit(solution)/shard_map/collect_x/pallas_call | solution.py:151
  80.3 4.1 %collect.1 = f32[32,16,4,128]{3,2,1,0:T(4,128)} custom-call(s32[192]{0:T(256)} %get-tuple-element.47.idx_ref, f32[129,16,128]{2,1,0:T(8,128)} %collect_x.1.acc_ref, f32[96,16,128]{2,1,0:T(8,128)} %copy-done.5, f32[96,16,128]{2,1,0:T(8,128)} %copy-done.6), custom_call_target="tpu_custom_call" | custom-call | flops 1000000 | bytes 5000000 | tf_op jit(solution)/shard_map/collect/pallas_call | solution.py:162
  84.4 9.3 %all-to-all-start = ((f32[32,16,4,128]{3,2,1,0:T(4,128)}), f32[32,16,4,128]{3,2,1,0:T(4,128)S(1)}, u32[]{:S(2)}, u32[]{:S(2)}) async-start(f32[32,16,4,128]{3,2,1,0:T(4,128)} %collect.1), calls=%async_computation | async-start | bytes 2097152 | tf_op jit(solution)/shard_map/all_to_all | solution.py:443
  96.5 18.6 %collective-permute-done.9.m1_ref = f32[8,136,128]{2,1,0:T(8,128)S(1)} collective-permute-done((f32[8,136,128]{2,1,0:T(8,128)S(1)}, f32[8,136,128]{2,1,0:T(8,128)S(1)}, u32[]{:S(2)}, u32[]{:S(2)}) %collective-permute-start.9) | collective-permute-done | bytes 557088 | tf_op jit(solution)/shard_map/ppermute | solution.py:28
  116.0 2.1 collective-permute-done.10.m3_ref
  118.2 3.5 %collective-permute-start.12 = (f32[4,136,128]{2,1,0:T(8,128)S(1)}, f32[4,136,128]{2,1,0:T(8,128)}, u32[]{:S(2)}, u32[]{:S(2)}) collective-permute-start(f32[4,136,128]{2,1,0:T(8,128)S(1)} %slice.9), channel_id=1, source_target_pairs={{0,24},{8,0},{16,8},{24,16},{32,56},{40,32},{48,40},{56,48},{64,88... | collective-permute-start | bytes 835592 | tf_op jit(solution)/shard_map/ppermute | solution.py:28
  125.4 2.8 %shard_map.95 = (f32[16,4,128]{2,1,0:T(4,128)}, f32[8,4,4,128]{3,2,1,0:T(4,128)}) custom-call(f32[32,16,4,128]{3,2,1,0:T(4,128)} %copy-done.1, bf16[16,128,256]{2,1,0:T(8,128)(2,1)} %get-tuple-element.27.bt_ref, f32[4,8,128]{2,1,0:T(8,128)} %get-tuple-element.28.par_ref), custom_call_target="tpu_custom_call" | custom-call | flops 100000000 | bytes 4000000 | tf_op jit(solution)/shard_map/pallas_call | solution.py:366
  128.2 6.7 %all-to-all-start.1 = ((f32[8,4,4,128]{3,2,1,0:T(4,128)}), f32[8,4,4,128]{3,2,1,0:T(4,128)S(1)}, u32[]{:S(2)}, u32[]{:S(2)}) async-start(f32[8,4,4,128]{3,2,1,0:T(4,128)} %get-tuple-element.30), calls=%async_computation.1 | async-start | bytes 131072 | tf_op jit(solution)/shard_map/all_to_all | solution.py:443
  134.9 2.0 collective-permute-done.15.refs_3_
  137.6 4.7 %chain_prep.1 = (bf16[32,128,256]{2,1,0:T(8,128)(2,1)}, bf16[32,128,256]{2,1,0:T(8,128)(2,1)}, f32[8,8,128]{2,1,0:T(8,128)}, bf16[16,128,256]{2,1,0:T(8,128)(2,1)}) custom-call(s32[1]{0:T(128)} %bitcast.6.me_ref, f32[8,136,128]{2,1,0:T(8,128)} %copy-done.2, f32[8,136,128]{2,1,0:T(8,128)} %copy-done.3, f32[8,136,128]{2,1,0:T(8,128)} %copy-done.4, ...), custom_call_target="tpu_custom_call" | custom-call | flops 1000000 | bytes 6000000 | tf_op jit(solution)/shard_map/chain_prep/pallas_call | solution.py:275
  142.9 4.3 %shard_map.96 = (f32[16,4,128]{2,1,0:T(4,128)}, f32[8,4,4,128]{3,2,1,0:T(4,128)}) custom-call(s32[1]{0:T(128)} %bitcast.5.me_ref, f32[16,4,128]{2,1,0:T(4,128)} %get-tuple-element.29.d_ref, f32[8,4,4,128]{3,2,1,0:T(4,128)} %copy-done.12, bf16[32,128,256]{2,1,0:T(8,128)(2,1)} %get-tuple-element.33.ct_ref, f32[8,8,128]{2,1,0:T(8,128)} %get-tuple-element.34.cpar_ref, ...), custom_call_target="tpu_custom_call" | custom-call | flops 100000000 | bytes 4000000 | tf_op jit(solution)/shard_map/pallas_call | solution.py:366
  147.3 15.0 %all_to_all.25.all_ref = f32[8,4,4,128]{3,2,1,0:T(4,128)} all-to-all(f32[8,4,4,128]{3,2,1,0:T(4,128)} %get-tuple-element.38), channel_id=1, replica_groups={{0,32,64,96,128,160,192,224},{8,40,72,104,136,168,200,232},{16,48,80,11..., dimensions={0} | all-to-all | bytes 131072 | tf_op jit(solution)/shard_map/all_to_all | solution.py:443
  162.3 4.7 %shard_map.97 = f32[32,16,4,128]{3,2,1,0:T(4,128)} custom-call(s32[1]{0:T(128)} %bitcast.5.me_ref, f32[16,4,128]{2,1,0:T(4,128)} %get-tuple-element.37.z_ref, f32[8,4,4,128]{3,2,1,0:T(4,128)} %all_to_all.25.all_ref, bf16[32,128,256]{2,1,0:T(8,128)(2,1)} %get-tuple-element.39.cn_ref, f32[8,8,128]{2,1,0:T(8,128)} %get-tuple-element.34.cpar_ref, ...), custom_call_target="tpu_custom_call" | custom-call | flops 100000000 | bytes 4000000 | tf_op jit(solution)/shard_map/pallas_call | solution.py:366
  167.0 4.7 %all-to-all-start.4 = ((f32[32,16,4,128]{3,2,1,0:T(4,128)}), f32[32,16,4,128]{3,2,1,0:T(4,128)S(1)}, u32[]{:S(2)}, u32[]{:S(2)}) async-start(f32[32,16,4,128]{3,2,1,0:T(4,128)} %shard_map.97), calls=%async_computation.4 | async-start | bytes 2097152 | tf_op jit(solution)/shard_map/all_to_all | solution.py:443
  172.4 21.5 %all-to-all-done.4.own_ref = f32[32,16,4,128]{3,2,1,0:T(4,128)S(1)} async-done(((f32[32,16,4,128]{3,2,1,0:T(4,128)}), f32[32,16,4,128]{3,2,1,0:T(4,128)S(1)}, u32[]{:S(2)}, u32[]{:S(2)}) %all-to-all-start.4) | async-done | bytes 1048608 | tf_op jit(solution)/shard_map/all_to_all | solution.py:443
  194.9 3.7 %pick.2 = (f32[96,16,128]{2,1,0:T(8,128)}, f32[96,16,128]{2,1,0:T(8,128)}) custom-call(s32[192]{0:T(256)} %and_select_fusion.5.idx_ref, f32[32,16,4,128]{3,2,1,0:T(4,128)} %copy-done), custom_call_target="tpu_custom_call" | custom-call | flops 1000000 | bytes 3000000 | tf_op jit(solution)/shard_map/pick/pallas_call | solution.py:393
  198.6 6.9 %collective-permute-start.16 = (f32[96,16,128]{2,1,0:T(8,128)}, f32[96,16,128]{2,1,0:T(8,128)S(1)}, u32[]{:S(2)}, u32[]{:S(2)}) collective-permute-start(f32[96,16,128]{2,1,0:T(8,128)} %get-tuple-element.41), channel_id=1, source_target_pairs={{0,4},{4,0},{1,5},{5,1},{2,6},{6,2},{3,7},{7,3},{8,12},{12,8},{9,1... | collective-permute-start | bytes 2359304 | tf_op jit(solution)/shard_map/ppermute | solution.py:37
  205.5 3.7 %pick.3 = (f32[96,16,128]{2,1,0:T(8,128)}, f32[96,16,128]{2,1,0:T(8,128)}) custom-call(s32[192]{0:T(256)} %get-tuple-element.46.idx_ref, f32[32,16,4,128]{3,2,1,0:T(4,128)} %copy-done), custom_call_target="tpu_custom_call" | custom-call | flops 1000000 | bytes 3000000 | tf_op jit(solution)/shard_map/pick/pallas_call | solution.py:393
  209.3 3.1 %collective-permute-start.17 = (f32[96,16,128]{2,1,0:T(8,128)}, f32[96,16,128]{2,1,0:T(8,128)S(1)}, u32[]{:S(2)}, u32[]{:S(2)}) collective-permute-start(f32[96,16,128]{2,1,0:T(8,128)} %get-tuple-element.42), channel_id=1, source_target_pairs={{0,1},{1,2},{2,3},{4,5},{5,6},{6,7},{8,9},{9,10},{10,11},{12,13},{... | collective-permute-start | bytes 2359304 | tf_op jit(solution)/shard_map/ppermute | solution.py:33
  215.7 13.8 %collective-permute-done.17.refs_2_ = f32[96,16,128]{2,1,0:T(8,128)S(1)} collective-permute-done((f32[96,16,128]{2,1,0:T(8,128)}, f32[96,16,128]{2,1,0:T(8,128)S(1)}, u32[]{:S(2)}, u32[]{:S(2)}) %collective-permute-start.17) | collective-permute-done | bytes 786464 | tf_op jit(solution)/shard_map/ppermute | solution.py:33
  229.5 3.8 %collective-permute-done.18.refs_3_ = f32[96,16,128]{2,1,0:T(8,128)S(1)} collective-permute-done((f32[96,16,128]{2,1,0:T(8,128)}, f32[96,16,128]{2,1,0:T(8,128)S(1)}, u32[]{:S(2)}, u32[]{:S(2)}) %collective-permute-start.18) | collective-permute-done | bytes 786464 | tf_op jit(solution)/shard_map/ppermute | solution.py:33
  234.2 11.1 %leaf_down.1 = f32[48,16,128]{2,1,0:T(8,128)} custom-call(s32[96]{0:T(128)} %or_select_fusion.slot_ref, f32[48,16,128]{2,1,0:T(8,128)} %get-tuple-element.23.mid_ref, f32[48,128,128]{2,1,0:T(8,128)} %bitcast.19, f32[48,2,128,128]{3,2,1,0:T(8,128)} %bitcast.17, f32[96,16,128]{2,1,0:T(8,128)} %get-tuple-element.40.refs_0_, f32[96,16,128]{2,1,0:T(8,128)} %copy-done.8, ...), custom_call_target="tpu_custom_call" | custom-call | flops 1000000000 | bytes 14000000 | tf_op jit(solution)/shard_map/leaf_down/pallas_call | solution.py:433
  (80 shorter events, 27.5 us)
Async XLA Ops:
  2.9 7.3 %collective-permute-start.6 = (f32[520,128]{1,0:T(8,128)}, f32[520,128]{1,0:T(8,128)S(1)}, u32[]{:S(2)}, u32[]{:S(2)}) collective-permute-start(f32[520,128]{1,0:T(8,128)} %get-tuple-element.26.p0_ref), channel_id=1, source_target_pairs={{0,8},{8,16},{16,24},{24,0},{32,40},{40,48},{48,56},{56,32},{64,72... | collective-permute-start | bytes 798728 | tf_op jit(solution)/shard_map/ppermute | solution.py:28
  4.9 14.2 %collective-permute-start.7 = (f32[520,128]{1,0:T(8,128)}, f32[520,128]{1,0:T(8,128)S(1)}, u32[]{:S(2)}, u32[]{:S(2)}) collective-permute-start(f32[520,128]{1,0:T(8,128)} %get-tuple-element.26.p0_ref), channel_id=1, source_target_pairs={{0,16},{8,24},{16,0},{24,8},{32,48},{40,56},{48,32},{56,40},{64,80... | collective-permute-start | bytes 798728 | tf_op jit(solution)/shard_map/ppermute | solution.py:28
  7.4 11.7 %collective-permute-start.8 = (f32[520,128]{1,0:T(8,128)}, f32[520,128]{1,0:T(8,128)S(1)}, u32[]{:S(2)}, u32[]{:S(2)}) collective-permute-start(f32[520,128]{1,0:T(8,128)} %get-tuple-element.26.p0_ref), channel_id=1, source_target_pairs={{0,24},{8,0},{16,8},{24,16},{32,56},{40,32},{48,40},{56,48},{64,88... | collective-permute-start | bytes 798728 | tf_op jit(solution)/shard_map/ppermute | solution.py:28
  9.4 60.7 %copy-start.14 = (s32[96]{0:T(128)}, s32[96]{0:T(128)S(1)}, u32[]{:S(2)}) copy-start(s32[96]{0:T(128)S(1)} %reshape_squeeze.3) | copy-start | bytes 1156
  10.2 8.9 %copy-start.17 = (f32[520,128]{1,0:T(8,128)}, f32[520,128]{1,0:T(8,128)S(1)}, u32[]{:S(2)}) copy-start(f32[520,128]{1,0:T(8,128)S(1)} %collective-permute-done.6.p1_ref) | copy-start | bytes 798724
  23.3 61.2 %all-to-all-start.2 = ((f32[8,136,128]{2,1,0:T(8,128)}), f32[8,136,128]{2,1,0:T(8,128)S(1)}, u32[]{:S(2)}, u32[]{:S(2)}) async-start(f32[8,136,128]{2,1,0:T(8,128)} %get-tuple-element.31), calls=%async_computation.2 | async-start | bytes 1114112 | tf_op jit(solution)/shard_map/all_to_all | solution.py:443
  44.1 31.1 %collective-permute-start.3 = (f32[96,16,128]{2,1,0:T(8,128)}, f32[96,16,128]{2,1,0:T(8,128)S(1)}, u32[]{:S(2)}, u32[]{:S(2)}) collective-permute-start(f32[96,16,128]{2,1,0:T(8,128)} %get-tuple-element.25), channel_id=1, source_target_pairs={{0,4},{4,0},{1,5},{5,1},{2,6},{6,2},{3,7},{7,3},{8,12},{12,8},{9,1... | collective-permute-start | bytes 2359304 | tf_op jit(solution)/shard_map/ppermute | solution.py:37
  46.0 33.1 %collective-permute-start.4 = (f32[96,16,128]{2,1,0:T(8,128)}, f32[96,16,128]{2,1,0:T(8,128)S(1)}, u32[]{:S(2)}, u32[]{:S(2)}) collective-permute-start(f32[96,16,128]{2,1,0:T(8,128)} %get-tuple-element.25), channel_id=1, source_target_pairs={{0,1},{1,2},{2,3},{4,5},{5,6},{6,7},{8,9},{9,10},{10,11},{12,13},{... | collective-permute-start | bytes 2359304 | tf_op jit(solution)/shard_map/ppermute | solution.py:33
  49.2 29.9 %collective-permute-start.5 = (f32[96,16,128]{2,1,0:T(8,128)}, f32[96,16,128]{2,1,0:T(8,128)S(1)}, u32[]{:S(2)}, u32[]{:S(2)}) collective-permute-start(f32[96,16,128]{2,1,0:T(8,128)} %get-tuple-element.25), channel_id=1, source_target_pairs={{1,0},{2,1},{3,2},{5,4},{6,5},{7,6},{9,8},{10,9},{11,10},{13,12},{... | collective-permute-start | bytes 2359304 | tf_op jit(solution)/shard_map/ppermute | solution.py:33
  50.5 24.1 %collective-permute-start = (s32[96]{0:T(128)S(1)}, s32[96]{0:T(128)S(1)}, u32[]{:S(2)}, u32[]{:S(2)}) collective-permute-start(s32[96]{0:T(128)S(1)} %reshape_squeeze.3), channel_id=1, source_target_pairs={{0,4},{4,0},{1,5},{5,1},{2,6},{6,2},{3,7},{7,3},{8,12},{12,8},{9,1... | collective-permute-start | bytes 1160 | tf_op jit(solution)/shard_map/ppermute | solution.py:37
  50.9 19.2 %collective-permute-start.2 = (s32[96]{0:T(128)S(1)}, s32[96]{0:T(128)S(1)}, u32[]{:S(2)}, u32[]{:S(2)}) collective-permute-start(s32[96]{0:T(128)S(1)} %reshape_squeeze.3), channel_id=1, source_target_pairs={{1,0},{2,1},{3,2},{5,4},{6,5},{7,6},{9,8},{10,9},{11,10},{13,12},{... | collective-permute-start | bytes 1160 | tf_op jit(solution)/shard_map/ppermute | solution.py:33
  70.1 3.8 %collective-permute-start.1 = (s32[96]{0:T(128)S(1)}, s32[96]{0:T(128)S(1)}, u32[]{:S(2)}, u32[]{:S(2)}) collective-permute-start(s32[96]{0:T(128)S(1)} %reshape_squeeze.3), channel_id=1, source_target_pairs={{0,1},{1,2},{2,3},{4,5},{5,6},{6,7},{8,9},{9,10},{10,11},{12,13},{... | collective-permute-start | bytes 1160 | tf_op jit(solution)/shard_map/ppermute | solution.py:33
  84.4 43.8 %copy-start.2 = (f32[8,136,128]{2,1,0:T(8,128)}, f32[8,136,128]{2,1,0:T(8,128)S(1)}, u32[]{:S(2)}) copy-start(f32[8,136,128]{2,1,0:T(8,128)S(1)} %all-to-all-done.2.m0_ref) | copy-start | bytes 1671172
  84.4 40.0 %all-to-all-start = ((f32[32,16,4,128]{3,2,1,0:T(4,128)}), f32[32,16,4,128]{3,2,1,0:T(4,128)S(1)}, u32[]{:S(2)}, u32[]{:S(2)}) async-start(f32[32,16,4,128]{3,2,1,0:T(4,128)} %collect.1), calls=%async_computation | async-start | bytes 2097152 | tf_op jit(solution)/shard_map/all_to_all | solution.py:443
  93.7 21.4 %collective-permute-start.9 = (f32[8,136,128]{2,1,0:T(8,128)S(1)}, f32[8,136,128]{2,1,0:T(8,128)S(1)}, u32[]{:S(2)}, u32[]{:S(2)}) collective-permute-start(f32[8,136,128]{2,1,0:T(8,128)S(1)} %all-to-all-done.2.m0_ref), channel_id=1, source_target_pairs={{0,8},{8,16},{16,24},{24,0},{32,40},{40,48},{48,56},{56,32},{64,72... | collective-permute-start | bytes 1671176 | tf_op jit(solution)/shard_map/ppermute | solution.py:28
  95.0 23.1 %collective-permute-start.10 = (f32[8,136,128]{2,1,0:T(8,128)S(1)}, f32[8,136,128]{2,1,0:T(8,128)S(1)}, u32[]{:S(2)}, u32[]{:S(2)}) collective-permute-start(f32[8,136,128]{2,1,0:T(8,128)S(1)} %all-to-all-done.2.m0_ref), channel_id=1, source_target_pairs={{0,24},{8,0},{16,8},{24,16},{32,56},{40,32},{48,40},{56,48},{64,88... | collective-permute-start | bytes 1671176 | tf_op jit(solution)/shard_map/ppermute | solution.py:28
  115.1 21.8 %copy-start.3 = (f32[8,136,128]{2,1,0:T(8,128)}, f32[8,136,128]{2,1,0:T(8,128)S(1)}, u32[]{:S(2)}) copy-start(f32[8,136,128]{2,1,0:T(8,128)S(1)} %collective-permute-done.9.m1_ref) | copy-start | bytes 1671172
  115.1 21.8 %collective-permute-start.11 = (f32[4,136,128]{2,1,0:T(8,128)S(1)}, f32[4,136,128]{2,1,0:T(8,128)S(1)}, u32[]{:S(2)}, u32[]{:S(2)}) collective-permute-start(f32[4,136,128]{2,1,0:T(8,128)S(1)} %slice.8), channel_id=1, source_target_pairs={{0,8},{8,16},{16,24},{24,0},{32,40},{40,48},{48,56},{56,32},{64,72... | collective-permute-start | bytes 835592 | tf_op jit(solution)/shard_map/ppermute | solution.py:28
  118.2 18.8 %copy-start.4 = (f32[8,136,128]{2,1,0:T(8,128)}, f32[8,136,128]{2,1,0:T(8,128)S(1)}, u32[]{:S(2)}) copy-start(f32[8,136,128]{2,1,0:T(8,128)S(1)} %collective-permute-done.10.m3_ref) | copy-start | bytes 1671172
  118.2 18.7 %collective-permute-start.12 = (f32[4,136,128]{2,1,0:T(8,128)S(1)}, f32[4,136,128]{2,1,0:T(8,128)}, u32[]{:S(2)}, u32[]{:S(2)}) collective-permute-start(f32[4,136,128]{2,1,0:T(8,128)S(1)} %slice.9), channel_id=1, source_target_pairs={{0,24},{8,0},{16,8},{24,16},{32,56},{40,32},{48,40},{56,48},{64,88... | collective-permute-start | bytes 835592 | tf_op jit(solution)/shard_map/ppermute | solution.py:28
  121.7 13.2 %collective-permute-start.13 = (f32[512,128]{1,0:T(8,128)}, f32[512,128]{1,0:T(8,128)}, u32[]{:S(2)}, u32[]{:S(2)}) collective-permute-start(f32[512,128]{1,0:T(8,128)} %get-tuple-element.32.refs_0_), channel_id=1, source_target_pairs={{0,8},{8,16},{16,24},{24,0},{32,40},{40,48},{48,56},{56,32},{64,72... | collective-permute-start | bytes 786440 | tf_op jit(solution)/shard_map/ppermute | solution.py:28
  121.7 13.2 %collective-permute-start.14 = (f32[512,128]{1,0:T(8,128)}, f32[512,128]{1,0:T(8,128)}, u32[]{:S(2)}, u32[]{:S(2)}) collective-permute-start(f32[512,128]{1,0:T(8,128)} %get-tuple-element.32.refs_0_), channel_id=1, source_target_pairs={{0,16},{8,24},{16,0},{24,8},{32,48},{40,56},{48,32},{56,40},{64,80... | collective-permute-start | bytes 786440 | tf_op jit(solution)/shard_map/ppermute | solution.py:28
  123.0 13.9 %collective-permute-start.15 = (f32[512,128]{1,0:T(8,128)}, f32[512,128]{1,0:T(8,128)}, u32[]{:S(2)}, u32[]{:S(2)}) collective-permute-start(f32[512,128]{1,0:T(8,128)} %get-tuple-element.32.refs_0_), channel_id=1, source_target_pairs={{0,24},{8,0},{16,8},{24,16},{32,56},{40,32},{48,40},{56,48},{64,88... | collective-permute-start | bytes 786440 | tf_op jit(solution)/shard_map/ppermute | solution.py:28
  128.2 14.1 %all-to-all-start.1 = ((f32[8,4,4,128]{3,2,1,0:T(4,128)}), f32[8,4,4,128]{3,2,1,0:T(4,128)S(1)}, u32[]{:S(2)}, u32[]{:S(2)}) async-start(f32[8,4,4,128]{3,2,1,0:T(4,128)} %get-tuple-element.30), calls=%async_computation.1 | async-start | bytes 131072 | tf_op jit(solution)/shard_map/all_to_all | solution.py:443
  166.9 4.7 %copy-start.13 = (s32[96]{0:T(128)S(1)}, s32[96]{0:T(128)}, u32[]{:S(2)}) copy-start(s32[96]{0:T(128)} %compare_select_fusion.6.idx_ref) | copy-start | bytes 1156
  166.9 4.7 %copy-start.15 = (s32[96]{0:T(128)S(1)}, s32[96]{0:T(128)}, u32[]{:S(2)}) copy-start(s32[96]{0:T(128)} %copy-done.14) | copy-start | bytes 1156
  167.0 46.8 %copy-start.16 = (s32[96]{0:T(128)S(1)}, s32[96]{0:T(128)}, u32[]{:S(2)}) copy-start(s32[96]{0:T(128)} %get-tuple-element.45) | copy-start | bytes 1156
  167.0 26.9 %all-to-all-start.4 = ((f32[32,16,4,128]{3,2,1,0:T(4,128)}), f32[32,16,4,128]{3,2,1,0:T(4,128)S(1)}, u32[]{:S(2)}, u32[]{:S(2)}) async-start(f32[32,16,4,128]{3,2,1,0:T(4,128)} %shard_map.97), calls=%async_computation.4 | async-start | bytes 2097152 | tf_op jit(solution)/shard_map/all_to_all | solution.py:443
  198.6 17.1 %collective-permute-start.16 = (f32[96,16,128]{2,1,0:T(8,128)}, f32[96,16,128]{2,1,0:T(8,128)S(1)}, u32[]{:S(2)}, u32[]{:S(2)}) collective-permute-start(f32[96,16,128]{2,1,0:T(8,128)} %get-tuple-element.41), channel_id=1, source_target_pairs={{0,4},{4,0},{1,5},{5,1},{2,6},{6,2},{3,7},{7,3},{8,12},{12,8},{9,1... | collective-permute-start | bytes 2359304 | tf_op jit(solution)/shard_map/ppermute | solution.py:37
  209.3 20.2 %collective-permute-start.17 = (f32[96,16,128]{2,1,0:T(8,128)}, f32[96,16,128]{2,1,0:T(8,128)S(1)}, u32[]{:S(2)}, u32[]{:S(2)}) collective-permute-start(f32[96,16,128]{2,1,0:T(8,128)} %get-tuple-element.42), channel_id=1, source_target_pairs={{0,1},{1,2},{2,3},{4,5},{5,6},{6,7},{8,9},{9,10},{10,11},{12,13},{... | collective-permute-start | bytes 2359304 | tf_op jit(solution)/shard_map/ppermute | solution.py:33
  212.4 20.9 %collective-permute-start.18 = (f32[96,16,128]{2,1,0:T(8,128)}, f32[96,16,128]{2,1,0:T(8,128)S(1)}, u32[]{:S(2)}, u32[]{:S(2)}) collective-permute-start(f32[96,16,128]{2,1,0:T(8,128)} %get-tuple-element.43), channel_id=1, source_target_pairs={{1,0},{2,1},{3,2},{5,4},{6,5},{7,6},{9,8},{10,9},{11,10},{13,12},{... | collective-permute-start | bytes 2359304 | tf_op jit(solution)/shard_map/ppermute | solution.py:33
  215.7 17.6 %copy-start.8 = (f32[96,16,128]{2,1,0:T(8,128)}, f32[96,16,128]{2,1,0:T(8,128)S(1)}, u32[]{:S(2)}) copy-start(f32[96,16,128]{2,1,0:T(8,128)S(1)} %collective-permute-done.16.refs_1_) | copy-start | bytes 2359300
  (11 other events, 12.5 us)
